TPU v7x, 512 devices: a whole 4x4x16 slice. The times are simulated.
512 devices in a mesh: row: 32 (over y, z_hi, core), col: 16 (over z_lo, x).
Axes of the slice: x: 4, y: 4, z: 16 (z_hi: 4, z_lo: 4; z = z_hi * 4 + z_lo), core: 2. Of those that a mesh axis runs over, the one named last changes fastest.
Arguments:
- trailing: bfloat16 [16384, 32768], P('row', 'col'), may hold values from -6 to 6
- col_u: bfloat16 [32, 512, 64], P('row', 'col'), may hold values from -6 to 6
- col_v: bfloat16 [32, 512, 64], P('row', 'col'), may hold values from -0.75 to 0.75
- row_u: bfloat16 [64, 512, 64], P('col', 'row'), may hold values from -6 to 6
- row_v: bfloat16 [64, 512, 64], P('col', 'row'), may hold values from -0.03125 to 0.03125
- diag_lower_inv: float32 [512, 512], replicated, may hold values from -0.176776695 to 1, as said below
- diag_upper_inv: float32 [512, 512], replicated, may hold values from -0.176776695 to 2, as said below
Outputs:
- schur: bfloat16 [16384, 32768], P('row', 'col')
Inputs may be any that keep to these rules, and one draw needn't show every extreme that they name: `diag_lower_inv`: lower triangular with unit diagonal. `diag_upper_inv`: upper triangular with diagonal entries between 0.5 and 2.
All inputs are finite; a program needn't handle non-finite values.
Results may differ from a plain program's by a relative error of at most 0.0054.
Values may be sent and summed in bfloat16 or wider, within the bound.
No kernel may reach another device: no remote copies, remote signals or barrier semaphores. Data moves between devices by JAX's collectives and lax.ppermute only.
A program may use at most 64 MiB of HBM per device.

v0:
```python
import jax
import jax.numpy as jnp
from jax import lax
from jax.sharding import PartitionSpec as P


def joined_along(tiles, dim):
    shape = list(tiles.shape[1:])
    shape[dim] *= tiles.shape[0]
    return jnp.moveaxis(tiles, 0, dim).reshape(shape)


def from_everyone(array, axis):
    length = lax.axis_size(axis)
    return lax.all_to_all(
        jnp.broadcast_to(array[None], (length, *array.shape)), axis, 0, 0, tiled=True
    )


def gathered_copies(array, axis, dim):
    return joined_along(from_everyone(array, axis), dim)


def in_one_piece(arrays, axis, dim, along):
    both = jnp.concatenate(arrays, axis=along)
    filled, at, gathered = (gathered_copies(both, axis, dim), 0, [])
    for a in arrays:
        gathered.append(lax.slice_in_dim(filled, at, at + a.shape[along], axis=along))
        at += a.shape[along]
    return tuple(gathered)


def side_by_side(arrays, axis, dim, along):
    both = jnp.concatenate(arrays, axis=along)
    filled, at, gathered = (lax.all_gather(both, axis, axis=dim, tiled=True), 0, [])
    for a in arrays:
        gathered.append(lax.slice_in_dim(filled, at, at + a.shape[along], axis=along))
        at += a.shape[along]
    return tuple(gathered)


def shards(trailing, col_u, col_v, row_u, row_v, diag_lower_inv, diag_upper_inv):
    highest = lax.Precision.HIGHEST
    whole_col_u, whole_col_v = in_one_piece((col_u, col_v), "col", 1, 0)
    left_v = jnp.einsum(
        "ba,tbr->tar", diag_upper_inv, whole_col_v.astype(jnp.float32), precision=highest
    )
    lower = jnp.einsum(
        "tpr,tar->tpa", whole_col_u.astype(jnp.float32), left_v, precision=highest
    ).astype(jnp.bfloat16)
    whole_row_u, whole_row_v = side_by_side((row_u, row_v), "row", 1, 0)
    right_u = jnp.einsum(
        "ab,tbr->tar", diag_lower_inv, whole_row_u.astype(jnp.float32), precision=highest
    )
    upper_flip = jnp.einsum(
        "tar,tqr->tqa", right_u, whole_row_v.astype(jnp.float32), precision=highest
    ).astype(jnp.bfloat16)
    order = lower.shape[2]
    lower_flat = lower.reshape(-1, order)
    upper_flat = upper_flip.reshape(-1, order)
    product = lax.dot_general(
        lower_flat, upper_flat, (((1,), (1,)), ((), ())), preferred_element_type=jnp.float32
    )
    return (trailing.astype(jnp.float32) - product).astype(jnp.bfloat16)


def solution(mesh):
    placed = (
        P("row", "col"),
        P("row", "col", None),
        P("row", "col", None),
        P("col", "row", None),
        P("col", "row", None),
        P(),
        P(),
    )
    return jax.shard_map(
        shards, mesh=mesh, in_specs=placed, out_specs=P("row", "col"), check_vma=False
    )
```

profile of v0, /device:TPU:1, one launch (start us, length us, event | category | flops | bytes accessed | tf_op | source)
XLA Modules:
  0.0 81.2 jit_solution(1611277147858840656)
XLA Ops:
  0.0 0.0 copy-start
  0.0 0.8 pad_maximum_fusion.1
  0.9 0.9 %reshape.26 = bf16[16,2,2048]{2,1,0:T(2,128)(2,1)} reshape(bf16[16,2,32,64]{3,2,1,0:T(8,128)(2,1)S(1)} %broadcast_in_dim.2) | data formatting | bytes 262144
  1.8 9.0 %all-to-all-start = ((bf16[16,2,2048]{2,1,0:T(2,128)(2,1)}), bf16[16,2,2048]{2,1,0:T(2,128)(2,1)S(1)}, u32[]{:S(2)}, u32[]{:S(2)}) async-start(bf16[16,2,2048]{2,1,0:T(2,128)(2,1)} %reshape.26), calls=%async_computation | async-start | bytes 262144 | tf_op jit(solution)/shard_map/all_to_all | solution.py:15
  10.8 0.7 pad_maximum_fusion
  11.6 61.1 %all_gather.3 = bf16[8,512,64]{2,0,1:T(8,128)(2,1)S(1)} all-gather(bf16[8,16,64]{2,0,1:T(8,128)(2,1)S(1)} %copy.10), channel_id=1, replica_groups=mesh['row'=32,'col'=16] {'row'}, dimensions={1}, use_global_device_ids=true | all-gather | bytes 540672 | tf_op jit(solution)/shard_map/all_gather | solution.py:35
  72.7 0.3 fusion.4
  73.0 0.0 copy-done
  73.0 1.0 %fusion = f32[4,64,512]{2,1,0:T(8,128)S(1)} fusion(f32[512,512]{1,0:T(8,128)S(1)} %copy-done, bf16[4,512,64]{2,0,1:T(4,128)(2,1)S(1)} %get-tuple-element.6), kind=kOutput, calls=%fused_computation.3 | convolution fusion | flops 805306368 | bytes 1835008 | tf_op jit(solution)/shard_map/ab,tbr->tar/dot_general | solution.py:52
  74.0 1.8 %convolution_convert_fusion = bf16[4,512,512]{2,1,0:T(8,128)(2,1)S(1)} fusion(f32[4,64,512]{2,1,0:T(8,128)S(1)} %fusion, bf16[4,512,64]{2,0,1:T(4,128)(2,1)S(1)} %get-tuple-element.5), kind=kOutput, calls=%fused_computation.1 | convolution fusion | flops 806354944 | bytes 2883584 | tf_op jit(solution)/shard_map/tar,tqr->tqa/dot_general | solution.py:55
  75.8 0.0 all-to-all-done
  75.8 0.2 reshape.27
  76.0 0.0 copy-start.1
  76.1 1.9 %fusion.6 = f32[64,512]{1,0:T(8,128)S(1)} fusion(bf16[512,64]{1,0:T(8,128)(2,1)S(1)} %bitcast.16, f32[512,512]{1,0:T(8,128)} %param.13), kind=kOutput, calls=%fused_computation.11 | convolution fusion | flops 201326592 | bytes 1245184 | tf_op jit(solution)/shard_map/ba,tbr->tar/dot_general | solution.py:45
  78.0 0.6 convolution_convert_fusion.1
  78.5 0.0 copy-done.1
  78.6 2.6 %subtract_convert_fusion = bf16[512,2048]{1,0:T(8,128)(2,1)} fusion(bf16[512,2048]{1,0:T(8,128)(2,1)S(1)} %copy-done.1, bf16[512,512]{1,0:T(8,128)(2,1)S(1)} %convolution_convert_fusion.1, bf16[2048,512]{1,0:T(8,128)(2,1)S(1)} %bitcast.14), kind=kOutput, calls=%fused_computation | convolution fusion | flops 1076887552 | bytes 6815744 | tf_op jit(solution)/shard_map/dot_general | solution.py:61
  (3 shorter events, 0.1 us)
Async XLA Ops:
  0.0 73.0 %copy-start = (f32[512,512]{1,0:T(8,128)S(1)}, f32[512,512]{1,0:T(8,128)}, u32[]{:S(2)}) copy-start(f32[512,512]{1,0:T(8,128)} %param.12) | copy-start | bytes 3145732
  1.8 74.1 %all-to-all-start = ((bf16[16,2,2048]{2,1,0:T(2,128)(2,1)}), bf16[16,2,2048]{2,1,0:T(2,128)(2,1)S(1)}, u32[]{:S(2)}, u32[]{:S(2)}) async-start(bf16[16,2,2048]{2,1,0:T(2,128)(2,1)} %reshape.26), calls=%async_computation | async-start | bytes 262144 | tf_op jit(solution)/shard_map/all_to_all | solution.py:15
  76.0 2.5 %copy-start.1 = (bf16[512,2048]{1,0:T(8,128)(2,1)S(1)}, bf16[512,2048]{1,0:T(8,128)(2,1)}, u32[]{:S(2)}) copy-start(bf16[512,2048]{1,0:T(8,128)(2,1)} %param.7) | copy-start | bytes 6291460
where the time goes:
time: 82.7 us; the launch traced here: 81.2 us
  blocking collectives  61.1 us (74%)
  starting transfers between devices  9.01 us (11%)
  matrix products  7.88 us (10%)
  other arithmetic  1.56 us (2%)
  local copies, waits for them, and re-layouts  1.53 us (2%)
    all_gather x1, blocking collectives, side_by_side(): lax.all_gather(both, axis, axis=dim, tiled=True)  61.1 us
    all_to_all x1, starting transfers between devices, from_everyone(): lax.all_to_all(jnp.broadcast_to(array[None], (length, *array.shape)), axi...  9.01 us
    dot_general x1, matrix products, shards(): lax.dot_general(lower_flat, upper_flat, (((1,), (1,)), ((), ())), preferr...  2.65 us
    dot_general x1, matrix products, shards(): jnp.einsum('ba,tbr->tar', diag_upper_inv, whole_col_v.astype(jnp.float32)...  1.88 us
    dot_general x1, matrix products, shards(): jnp.einsum('tar,tqr->tqa', right_u, whole_row_v.astype(jnp.float32), prec...  1.79 us
  transfers between devices with their start and end apart: 1, of which 0 were waited for; matrix products, arithmetic and copies ran while one was open for 5% of the time, Pallas kernels for 0%

commit v1 on v0

v1 whole, which is shorter than its diff:
```python
import jax
import jax.numpy as jnp
from jax import lax
from jax.experimental import pallas as pl
from jax.experimental.pallas import tpu as pltpu
from jax.sharding import Mesh, PartitionSpec as P

Y, ZH, CORE, ZL, X = 4, 4, 2, 4, 4
ROW, COL = ("y", "zh", "core"), ("zl", "x")
B, R = 512, 64
F32, BF16 = jnp.float32, jnp.bfloat16


def split(x):
    hi = x.astype(BF16)
    return hi, (x - hi.astype(F32)).astype(BF16)


def dot(a, b, dims=((1,), (0,))):
    return lax.dot_general(a, b, (dims, ((), ())), preferred_element_type=F32)


def pack_kernel(ru_ref, rv_ref, cu_ref, cv_ref, row_ref, cols_hbm, buf, sem):
    buf[:, :R] = cu_ref[0]
    buf[:, R:] = cv_ref[0]
    copies = [
        pltpu.make_async_copy(buf, cols_hbm.at[k], sem.at[k]) for k in range(ZL * X)
    ]
    for c in copies:
        c.start()
    row_ref[:, :R] = ru_ref[...].reshape(64, R)
    row_ref[:, R:] = rv_ref[...].reshape(64, R)
    for c in copies:
        c.wait()


def left_kernel(col_ref, upper_ref, lower_ref, q_ref, uu_ref):
    col = col_ref[...].reshape(B, 2 * R)
    u = col[:, :R]
    uu_ref[:, :R] = u
    uu_ref[:, R:] = u
    v = col[:, R:]
    dims = ((0,), (0,))
    up_hi, up_lo = split(upper_ref[...])
    left = dot(v, up_hi, dims) + dot(v, up_lo, dims)
    left_hi, left_lo = split(left)
    low_hi, low_lo = split(lower_ref[...])
    q = dot(left_hi, low_hi) + dot(left_lo, low_hi) + dot(left_hi, low_lo)
    q_hi, q_lo = split(q)
    q_ref[:R] = q_hi
    q_ref[R:] = q_lo


def schur_kernel(x_ref, q_ref, uu_ref, t_hbm, o_hbm, tbuf, obuf, tsem, osem):
    tiles = 4
    fetch = [
        pltpu.make_async_copy(t_hbm.at[:, pl.ds(j * B, B)], tbuf.at[j], tsem.at[j])
        for j in range(tiles)
    ]
    for f in fetch:
        f.start()
    order = [(c, y, z) for y in range(Y) for z in range(ZH) for c in range(CORE)]
    xs = [
        jnp.concatenate([x_ref[c, y, z, j * 16 : (j + 1) * 16, :] for c, y, z in order], axis=0)
        for j in range(tiles)
    ]
    q = q_ref[...]
    keep = lax.broadcasted_iota(jnp.int32, (R, 2 * R), 1) >= R
    ms = [dot(q, x) for x in xs]
    ws = []
    for x, m in zip(xs, ms, strict=True):
        m = jnp.where(keep, pltpu.roll(m[:R] + m[R:], R, 1), 0.0)
        w = dot(jnp.concatenate(split(m), axis=0), x, ((1,), (1,)))
        ws.append(jnp.concatenate(split(w[:R] + w[R:]), axis=0))
    uu = uu_ref[...]
    stores = []
    for j in range(tiles):
        p = dot(uu, ws[j])
        fetch[j].wait()
        obuf[j] = (tbuf[j].astype(F32) - p).astype(BF16)
        s = pltpu.make_async_copy(obuf.at[j], o_hbm.at[:, pl.ds(j * B, B)], osem.at[j])
        s.start()
        stores.append(s)
    for s in stores:
        s.wait()


def on_chip(*arrays):
    return tuple(pltpu.with_memory_space_constraint(a, pltpu.VMEM) for a in arrays)


def shards(trailing, col_u, col_v, row_u, row_v, diag_lower_inv, diag_upper_inv):
    vmem = pl.BlockSpec(memory_space=pltpu.VMEM)
    hbm = pl.BlockSpec(memory_space=pl.ANY)
    row, col_sends = pl.pallas_call(
        pack_kernel,
        in_specs=[vmem] * 4,
        out_specs=(vmem, hbm),
        out_shape=(pltpu.VMEM((64, 128), BF16), pltpu.HBM((ZL * X, 32, 128), BF16)),
        scratch_shapes=[pltpu.VMEM((32, 128), BF16), pltpu.SemaphoreType.DMA((ZL * X,))],
        name="pack",
    )(row_u, row_v, col_u, col_v)
    cols = lax.all_to_all(col_sends, COL, 0, 0, tiled=True)
    over_z = lax.all_gather(row, "zh", axis=0, tiled=False)
    over_z, cols = lax.optimization_barrier((over_z, cols))
    over_y = lax.all_to_all(
        jnp.broadcast_to(over_z[None], (Y, *over_z.shape)), "y", 0, 0, tiled=True
    )
    everything = lax.all_gather(over_y, "core", axis=0, tiled=False)
    q, uu = pl.pallas_call(
        left_kernel,
        in_specs=[vmem] * 3,
        out_specs=(vmem, vmem),
        out_shape=(pltpu.VMEM((2 * R, B), BF16), pltpu.VMEM((B, 2 * R), BF16)),
        name="left",
    )(*on_chip(cols), diag_upper_inv, diag_lower_inv)
    return pl.pallas_call(
        schur_kernel,
        in_specs=[vmem] * 3 + [hbm],
        out_specs=hbm,
        out_shape=jax.ShapeDtypeStruct((B, 4 * B), BF16),
        scratch_shapes=[
            pltpu.VMEM((4, B, B), BF16),
            pltpu.VMEM((4, B, B), BF16),
            pltpu.SemaphoreType.DMA((4,)),
            pltpu.SemaphoreType.DMA((4,)),
        ],
        name="schur",
    )(*on_chip(everything.reshape(CORE, Y, ZH, 64, 128), q, uu), trailing)


def solution(mesh):
    parts = Mesh(mesh.devices.reshape(Y, ZH, CORE, ZL, X), ROW + COL)
    placed = (
        P(ROW, COL),
        P(ROW, COL, None),
        P(ROW, COL, None),
        P(COL, ROW, None),
        P(COL, ROW, None),
        P(),
        P(),
    )
    return jax.shard_map(
        shards, mesh=parts, in_specs=placed, out_specs=P(ROW, COL), check_vma=False
    )
```

time: 82.7 us -> 52.5 us (0.63); the launches traced: 81.2 us -> 52.1 us
  blocking collectives: 61.1 us -> 27.2 us
  matrix products: 7.88 us -> 0 us
  Pallas kernels: 0 us -> 7.7 us
  starting transfers between devices: 9.01 us -> 13.2 us
  waiting for transfers between devices: 0.01 us -> 3.23 us
  other arithmetic: 1.56 us -> 0 us
    all_gather x1 -> x2, blocking collectives: 61.1 us -> 27.2 us  [the longest x1 20.1 us: shards(): over_z = lax.all_gather(row, 'zh', axis=0, tiled=False)]
    dot_general x5 -> x0, matrix products: 7.88 us -> none  [the longest x1 2.65 us: shards(): lax.dot_general(lower_flat, upper_flat, (((1,), (1,)), ((), ())), preferr...]
    pallas_call x0 -> x3, Pallas kernels: none -> 7.7 us  [the longest x1 3.79 us: shards(): pl.pallas_call(schur_kernel, in_specs=[vmem] * 3 + [hbm], out_specs=hbm,...]
    all_to_all x1 -> x2, starting transfers between devices: 9.01 us -> 13.2 us  [the longest x1 9.03 us: shards(): cols = lax.all_to_all(col_sends, COL, 0, 0, tiled=True)]
    all_to_all x1 -> x2, waiting for transfers between devices: 0.01 us -> 3.23 us  [the longest x1 3.22 us: shards(): lax.all_to_all(jnp.broadcast_to(over_z[None], (Y, *over_z.shape)), 'y', 0...]
    concatenate x2 -> x0, other arithmetic: 1.56 us -> none  [the longest x1 0.81 us: in_one_piece(): both = jnp.concatenate(arrays, axis=along)]
    unnamed x6 -> x0, local copies, waits for them, and re-layouts: 1.12 us -> none
  transfers between devices with their start and end apart: 1 -> 2, of which waited for: 0 -> 1; matrix products, arithmetic and copies ran while one was open for 5% -> 0% of each run, Pallas kernels for 0% -> 4%
where the time goes in v1:
time: 52.5 us; the launch traced here: 52.1 us
  blocking collectives  27.2 us (52%)
  starting transfers between devices  13.2 us (25%)
  Pallas kernels  7.7 us (15%)
  waiting for transfers between devices  3.23 us (6%)
  local copies, waits for them, and re-layouts  0.76 us (1%)
    all_gather x1, blocking collectives, shards(): over_z = lax.all_gather(row, 'zh', axis=0, tiled=False)  20.1 us
    all_to_all x1, starting transfers between devices, shards(): cols = lax.all_to_all(col_sends, COL, 0, 0, tiled=True)  9.03 us
    all_gather x1, blocking collectives, shards(): everything = lax.all_gather(over_y, 'core', axis=0, tiled=False)  7.11 us
    all_to_all x1, starting transfers between devices, shards(): lax.all_to_all(jnp.broadcast_to(over_z[None], (Y, *over_z.shape)), 'y', 0...  4.18 us
    pallas_call x1, Pallas kernels, shards(): pl.pallas_call(schur_kernel, in_specs=[vmem] * 3 + [hbm], out_specs=hbm,...  3.79 us
    all_to_all x1, waiting for transfers between devices, shards(): lax.all_to_all(jnp.broadcast_to(over_z[None], (Y, *over_z.shape)), 'y', 0...  3.22 us
    pallas_call x1, Pallas kernels, shards(): pl.pallas_call(left_kernel, in_specs=[vmem] * 3, out_specs=(vmem, vmem),...  2.3 us
    pallas_call x1, Pallas kernels, shards(): pl.pallas_call(pack_kernel, in_specs=[vmem] * 4, out_specs=(vmem, hbm), o...  1.61 us
  transfers between devices with their start and end apart: 2, of which 1 were waited for; matrix products, arithmetic and copies ran while one was open for 0% of the time, Pallas kernels for 4%

profile of v1, /device:TPU:1, one launch (start us, length us, event | category | flops | bytes accessed | tf_op | source)
XLA Modules:
  0.0 52.1 jit_solution(17451924513584312686)
XLA Ops:
  0.0 1.6 %pack.1 = (bf16[64,128]{1,0:T(8,128)(2,1)S(1)}, bf16[16,32,128]{2,1,0:T(8,128)(2,1)}) custom-call(bf16[4,16,64]{2,1,0:T(8,128)(2,1)} %ru_ref.1, bf16[4,16,64]{2,1,0:T(8,128)(2,1)} %rv_ref.1, bf16[1,32,64]{2,1,0:T(8,128)(2,1)} %cu_ref.1, bf16[1,32,64]{2,1,0:T(8,128)(2,1)} %cv_ref.1), custom_call_target="tpu_custom_call" | custom-call | tf_op jit(solution)/shard_map/pack/pallas_call | solution.py:95
  1.6 9.0 %all-to-all-start = ((bf16[16,32,128]{2,1,0:T(8,128)(2,1)}), bf16[16,32,128]{2,1,0:T(8,128)(2,1)S(1)}, u32[]{:S(2)}, u32[]{:S(2)}) async-start(bf16[16,32,128]{2,1,0:T(8,128)(2,1)} %get-tuple-element.12), calls=%async_computation | async-start | bytes 262144 | tf_op jit(solution)/shard_map/all_to_all | solution.py:103
  10.7 20.1 %all-gather = bf16[256,128]{1,0:T(8,128)(2,1)S(1)} all-gather(bf16[64,128]{1,0:T(8,128)(2,1)S(1)} %get-tuple-element.11), channel_id=2, replica_groups=mesh['y'=4,'zh'=4,'core'=2,'zl'=4,'x'=4] {'zh'}, dimensions={0}, use_global_device_ids=true | all-gather | bytes 81920 | tf_op jit(solution)/shard_map/all_gather | solution.py:104
  30.8 0.0 all-to-all-done.col_ref
  30.8 0.8 %broadcast_in_dim.2 = bf16[4,4,64,128]{3,2,1,0:T(8,128)(2,1)} broadcast(bf16[4,64,128]{2,1,0:T(8,128)(2,1)S(1)} %bitcast.3), dimensions={1,2,3} | broadcast | bytes 327680 | tf_op jit(solution)/shard_map/broadcast_in_dim | solution.py:107
  31.5 4.2 %all-to-all-start.1 = ((bf16[4,4,64,128]{3,2,1,0:T(8,128)(2,1)}), bf16[4,4,64,128]{3,2,1,0:T(8,128)(2,1)S(1)}, u32[]{:S(2)}, u32[]{:S(2)}) async-start(bf16[4,4,64,128]{3,2,1,0:T(8,128)(2,1)} %broadcast_in_dim.2), calls=%async_computation.1 | async-start | bytes 524288 | tf_op jit(solution)/shard_map/all_to_all | solution.py:106
  35.7 2.3 %left.1 = (bf16[128,512]{1,0:T(8,128)(2,1)S(1)}, bf16[512,128]{1,0:T(8,128)(2,1)S(1)}) custom-call(bf16[16,32,128]{2,1,0:T(8,128)(2,1)S(1)} %all-to-all-done.col_ref, f32[512,512]{1,0:T(8,128)} %upper_ref.1, f32[512,512]{1,0:T(8,128)} %lower_ref.1), custom_call_target="tpu_custom_call" | custom-call | tf_op jit(solution)/shard_map/left/pallas_call | solution.py:110
  38.0 3.2 %all-to-all-done.1 = bf16[4,4,64,128]{3,2,1,0:T(8,128)(2,1)S(1)} async-done(((bf16[4,4,64,128]{3,2,1,0:T(8,128)(2,1)}), bf16[4,4,64,128]{3,2,1,0:T(8,128)(2,1)S(1)}, u32[]{:S(2)}, u32[]{:S(2)}) %all-to-all-start.1) | async-done | bytes 262176 | tf_op jit(solution)/shard_map/all_to_all | solution.py:106
  41.2 7.1 %all-gather.1 = bf16[8,4,64,128]{3,2,1,0:T(8,128)(2,1)S(1)} all-gather(bf16[4,4,64,128]{3,2,1,0:T(8,128)(2,1)S(1)} %all-to-all-done.1), channel_id=3, replica_groups=mesh['y'=4,'zh'=4,'core'=2,'zl'=4,'x'=4] {'core'}, dimensions={0}, use_global_device_ids=true | all-gather | bytes 786432 | tf_op jit(solution)/shard_map/all_gather | solution.py:109
  48.4 3.8 %schur.1 = bf16[512,2048]{1,0:T(8,128)(2,1)} custom-call(bf16[2,4,4,64,128]{4,3,2,1,0:T(8,128)(2,1)S(1)} %bitcast.2, bf16[128,512]{1,0:T(8,128)(2,1)S(1)} %get-tuple-element.15.q_ref, bf16[512,128]{1,0:T(8,128)(2,1)S(1)} %get-tuple-element.16.uu_ref, bf16[512,2048]{1,0:T(8,128)(2,1)} %t_hbm.1), custom_call_target="tpu_custom_call" | custom-call | tf_op jit(solution)/shard_map/schur/pallas_call | solution.py:117
Async XLA Ops:
  1.6 29.2 %all-to-all-start = ((bf16[16,32,128]{2,1,0:T(8,128)(2,1)}), bf16[16,32,128]{2,1,0:T(8,128)(2,1)S(1)}, u32[]{:S(2)}, u32[]{:S(2)}) async-start(bf16[16,32,128]{2,1,0:T(8,128)(2,1)} %get-tuple-element.12), calls=%async_computation | async-start | bytes 262144 | tf_op jit(solution)/shard_map/all_to_all | solution.py:103
  31.5 9.7 %all-to-all-start.1 = ((bf16[4,4,64,128]{3,2,1,0:T(8,128)(2,1)}), bf16[4,4,64,128]{3,2,1,0:T(8,128)(2,1)S(1)}, u32[]{:S(2)}, u32[]{:S(2)}) async-start(bf16[4,4,64,128]{3,2,1,0:T(8,128)(2,1)} %broadcast_in_dim.2), calls=%async_computation.1 | async-start | bytes 524288 | tf_op jit(solution)/shard_map/all_to_all | solution.py:106

commit v2 on v1

v2 whole, which is shorter than its diff:
```python
import jax
import jax.numpy as jnp
from jax import lax
from jax.experimental import pallas as pl
from jax.experimental.pallas import tpu as pltpu
from jax.sharding import Mesh, PartitionSpec as P

Y, ZH, CORE, ZL, X = 4, 4, 2, 4, 4
ROW, COL = ("y", "zh", "core"), ("zl", "x")
B, R = 512, 64
F32, BF16 = jnp.float32, jnp.bfloat16


def split(x):
    hi = x.astype(BF16)
    return hi, (x - hi.astype(F32)).astype(BF16)


def dot(a, b, dims=((1,), (0,))):
    return lax.dot_general(a, b, (dims, ((), ())), preferred_element_type=F32)


def pack_row_kernel(u_ref, v_ref, row_ref):
    row_ref[:, :R] = u_ref[...].reshape(64, R)
    row_ref[:, R:] = v_ref[...].reshape(64, R)


def pack_col_kernel(u_ref, v_ref, row_ref, cols_hbm, buf, sem):
    buf[:, :R] = u_ref[0]
    buf[:, R:] = v_ref[0]
    copies = [
        pltpu.make_async_copy(buf, cols_hbm.at[k], sem.at[k]) for k in range(ZL * X)
    ]
    for c in copies:
        c.start()
    for c in copies:
        c.wait()


def fan_kernel(own_ref, first_ref, other_ref, sends_hbm, sem):
    copies = []
    for y in range(Y):
        to = sends_hbm.at[y]
        copies += [
            pltpu.make_async_copy(own_ref, to.at[0], sem.at[y, 0]),
            pltpu.make_async_copy(first_ref, to.at[1], sem.at[y, 1]),
            pltpu.make_async_copy(other_ref, to.at[pl.ds(2, 2)], sem.at[y, 2]),
        ]
    for c in copies:
        c.start()
    for c in copies:
        c.wait()


def left_kernel(col_ref, upper_ref, lower_ref, t_hbm, q_ref, uu_ref, *rest):
    held, sem = rest[:-1], rest[-1]
    fetch = [
        pltpu.make_async_copy(t_hbm.at[:, pl.ds(j * B, B)], h, sem.at[j])
        for j, h in enumerate(held)
    ]
    for f in fetch:
        f.start()
    col = col_ref[...].reshape(B, 2 * R)
    u = col[:, :R]
    uu_ref[:, :R] = u
    uu_ref[:, R:] = u
    v = col[:, R:]
    dims = ((0,), (0,))
    up_hi, up_lo = split(upper_ref[...])
    left = dot(v, up_hi, dims) + dot(v, up_lo, dims)
    left_hi, left_lo = split(left)
    low_hi, low_lo = split(lower_ref[...])
    q = dot(left_hi, low_hi) + dot(left_lo, low_hi) + dot(left_hi, low_lo)
    q_hi, q_lo = split(q)
    q_ref[:R] = q_hi
    q_ref[R:] = q_lo
    for f in fetch:
        f.wait()


def schur_kernel(me_ref, x_ref, q_ref, uu_ref, t0_ref, t1_ref, t2_ref, t3_ref, o_hbm, obuf, osem):
    held = (t0_ref, t1_ref, t2_ref, t3_ref)
    tiles = len(held)
    me = me_ref[0]
    slot = [me ^ z for z in range(ZH)]
    order = [(c, y, z) for y in range(Y) for z in range(ZH) for c in range(CORE)]
    xs = [
        jnp.concatenate([x_ref[c, y, slot[z], j * 16 : (j + 1) * 16, :] for c, y, z in order], axis=0)
        for j in range(tiles)
    ]
    q = q_ref[...]
    keep = lax.broadcasted_iota(jnp.int32, (R, 2 * R), 1) >= R
    ms = [dot(q, x) for x in xs]
    ws = []
    for x, m in zip(xs, ms, strict=True):
        m = jnp.where(keep, pltpu.roll(m[:R] + m[R:], R, 1), 0.0)
        w = dot(jnp.concatenate(split(m), axis=0), x, ((1,), (1,)))
        ws.append(jnp.concatenate(split(w[:R] + w[R:]), axis=0))
    uu = uu_ref[...]
    stores = []
    for j in range(tiles):
        p = dot(uu, ws[j])
        obuf[j] = (held[j][...].astype(F32) - p).astype(BF16)
        s = pltpu.make_async_copy(obuf.at[j], o_hbm.at[:, pl.ds(j * B, B)], osem.at[j])
        s.start()
        stores.append(s)
    for s in stores:
        s.wait()


def on_chip(*arrays):
    return tuple(pltpu.with_memory_space_constraint(a, pltpu.VMEM) for a in arrays)


def shards(trailing, col_u, col_v, row_u, row_v, diag_lower_inv, diag_upper_inv):
    vmem = pl.BlockSpec(memory_space=pltpu.VMEM)
    hbm = pl.BlockSpec(memory_space=pl.ANY)
    row = pl.pallas_call(
        pack_row_kernel,
        in_specs=[vmem] * 2,
        out_specs=vmem,
        out_shape=pltpu.VMEM((64, 128), BF16),
        name="pack_row",
    )(row_u, row_v)
    col_sends = pl.pallas_call(
        pack_col_kernel,
        in_specs=[vmem] * 3,
        out_specs=hbm,
        out_shape=pltpu.HBM((ZL * X, 32, 128), BF16),
        scratch_shapes=[pltpu.VMEM((32, 128), BF16), pltpu.SemaphoreType.DMA((ZL * X,))],
        name="pack_col",
    )(col_u, col_v, *on_chip(row))
    cols = lax.all_to_all(col_sends, COL, 0, 0, tiled=True)
    first = lax.ppermute(row, "zh", [(k, k ^ 1) for k in range(ZH)])
    pair = jnp.stack([first, row])
    other = lax.ppermute(pair, "zh", [(k, k ^ 3) for k in range(ZH)])
    sends = pl.pallas_call(
        fan_kernel,
        in_specs=[vmem] * 3,
        out_specs=hbm,
        out_shape=pltpu.HBM((Y, ZH, 64, 128), BF16),
        scratch_shapes=[pltpu.SemaphoreType.DMA((Y, 3))],
        cost_estimate=pl.CostEstimate(flops=4_000_000_000, transcendentals=0, bytes_accessed=1 << 18),
        name="fan",
    )(*on_chip(row, first, other))
    sends, cols = lax.optimization_barrier((sends, cols))
    over_y = lax.all_to_all(sends, "y", 0, 0, tiled=True)
    everything = lax.all_gather(over_y, "core", axis=0, tiled=False)
    q, uu, *held = pl.pallas_call(
        left_kernel,
        in_specs=[vmem] * 3 + [hbm],
        out_specs=(vmem,) * 6,
        out_shape=(
            pltpu.VMEM((2 * R, B), BF16),
            pltpu.VMEM((B, 2 * R), BF16),
            *[pltpu.VMEM((B, B), BF16)] * 4,
        ),
        scratch_shapes=[pltpu.SemaphoreType.DMA((4,))],
        name="left",
    )(*on_chip(cols), diag_upper_inv, diag_lower_inv, trailing)
    return pl.pallas_call(
        schur_kernel,
        in_specs=[pl.BlockSpec(memory_space=pltpu.SMEM)] + [vmem] * 7,
        out_specs=hbm,
        out_shape=jax.ShapeDtypeStruct((B, 4 * B), BF16),
        scratch_shapes=[
            pltpu.VMEM((4, B, B), BF16),
            pltpu.SemaphoreType.DMA((4,)),
        ],
        name="schur",
    )(lax.axis_index("zh")[None], *on_chip(everything.reshape(CORE, Y, ZH, 64, 128), q, uu, *held))


def solution(mesh):
    parts = Mesh(mesh.devices.reshape(Y, ZH, CORE, ZL, X), ROW + COL)
    placed = (
        P(ROW, COL),
        P(ROW, COL, None),
        P(ROW, COL, None),
        P(COL, ROW, None),
        P(COL, ROW, None),
        P(),
        P(),
    )
    return jax.shard_map(
        shards, mesh=parts, in_specs=placed, out_specs=P(ROW, COL), check_vma=False
    )
```

time: 52.5 us -> 47.6 us (0.907)
  blocking collectives: 27.2 us -> 5.32 us
  starting transfers between devices: 13.2 us -> 28.1 us
  waiting for transfers between devices: 3.23 us -> 5.08 us
  local copies, waits for them, and re-layouts: 0.76 us -> 0 us
  Pallas kernels: 7.7 us -> 8.41 us
    all_gather x1 -> x0, blocking collectives: 20.1 us -> none  [shards(): over_z = lax.all_gather(row, 'zh', axis=0, tiled=False)]
    ppermute x0 -> x2, starting transfers between devices: none -> 15.8 us  [the longest x1 9.64 us: shards(): first = lax.ppermute(row, 'zh', [(k, k ^ 1) for k in range(ZH)])]
    ppermute x0 -> x2, waiting for transfers between devices: none -> 2.74 us  [the longest x1 2.73 us: shards(): other = lax.ppermute(pair, 'zh', [(k, k ^ 3) for k in range(ZH)])]
    all_gather x1, blocking collectives: 7.11 us -> 5.32 us  [shards(): everything = lax.all_gather(over_y, 'core', axis=0, tiled=False)]
    all_to_all x1, waiting for transfers between devices: 3.22 us -> 2.34 us  [shards(): over_y = lax.all_to_all(sends, 'y', 0, 0, tiled=True)]
    all_to_all x1, starting transfers between devices: 9.03 us -> 8.2 us  [shards(): cols = lax.all_to_all(col_sends, COL, 0, 0, tiled=True)]
    broadcast_in_dim x1 -> x0, local copies, waits for them, and re-layouts: 0.76 us -> none  [shards(): jnp.broadcast_to(over_z[None], (Y, *over_z.shape))]
    pallas_call x3 -> x5, Pallas kernels: 7.7 us -> 8.41 us  [the longest x1 3.18 us: shards(): pl.pallas_call(left_kernel, in_specs=[vmem] * 3 + [hbm], out_specs=(vmem,...]
  transfers between devices with their start and end apart: 2 -> 4, of which waited for: 1 -> 2; matrix products, arithmetic and copies ran while one was open for 0% -> 0% of each run, Pallas kernels for 4% -> 12%
where the time goes in v2:
time: 47.6 us; the launch traced here: 47 us
  starting transfers between devices  28.1 us (59%)
  Pallas kernels  8.41 us (18%)
  blocking collectives  5.32 us (11%)
  waiting for transfers between devices  5.08 us (11%)
    ppermute x1, starting transfers between devices, shards(): first = lax.ppermute(row, 'zh', [(k, k ^ 1) for k in range(ZH)])  9.64 us
    all_to_all x1, starting transfers between devices, shards(): cols = lax.all_to_all(col_sends, COL, 0, 0, tiled=True)  8.2 us
    ppermute x1, starting transfers between devices, shards(): other = lax.ppermute(pair, 'zh', [(k, k ^ 3) for k in range(ZH)])  6.12 us
    all_gather x1, blocking collectives, shards(): everything = lax.all_gather(over_y, 'core', axis=0, tiled=False)  5.32 us
    all_to_all x1, starting transfers between devices, shards(): over_y = lax.all_to_all(sends, 'y', 0, 0, tiled=True)  4.2 us
    pallas_call x1, Pallas kernels, shards(): pl.pallas_call(left_kernel, in_specs=[vmem] * 3 + [hbm], out_specs=(vmem,...  3.18 us
    ppermute x1, waiting for transfers between devices, shards(): other = lax.ppermute(pair, 'zh', [(k, k ^ 3) for k in range(ZH)])  2.73 us
    all_to_all x1, waiting for transfers between devices, shards(): over_y = lax.all_to_all(sends, 'y', 0, 0, tiled=True)  2.34 us
  transfers between devices with their start and end apart: 4, of which 2 were waited for; matrix products, arithmetic and copies ran while one was open for 0% of the time, Pallas kernels for 12%

profile of v2, /device:TPU:1, one launch (start us, length us, event | category | flops | bytes accessed | tf_op | source)
XLA Modules:
  0.0 47.0 jit_solution(12118149868749907839)
XLA Ops:
  0.0 0.8 %pack_row.1.own_ref.row_ref = bf16[64,128]{1,0:T(8,128)(2,1)S(1)} custom-call(bf16[4,16,64]{2,1,0:T(8,128)(2,1)} %u_ref.2, bf16[4,16,64]{2,1,0:T(8,128)(2,1)} %v_ref.2), custom_call_target="tpu_custom_call" | custom-call | tf_op jit(solution)/shard_map/pack_row/pallas_call | solution.py:118
  0.8 9.6 %collective-permute-start = (bf16[64,128]{1,0:T(8,128)(2,1)S(1)}, bf16[64,128]{1,0:T(8,128)(2,1)S(1)}, u32[]{:S(2)}, u32[]{:S(2)}) collective-permute-start(bf16[64,128]{1,0:T(8,128)(2,1)S(1)} %pack_row.1.own_ref.row_ref), channel_id=1, source_target_pairs={{0,32},{32,0},{64,96},{96,64},{1,33},{33,1},{65,97},{97,65},{2,34}... | collective-permute-start | bytes 49160 | tf_op jit(solution)/shard_map/ppermute | solution.py:134
  10.5 1.6 %pack_col.1 = bf16[16,32,128]{2,1,0:T(8,128)(2,1)} custom-call(bf16[1,32,64]{2,1,0:T(8,128)(2,1)} %u_ref.3, bf16[1,32,64]{2,1,0:T(8,128)(2,1)} %v_ref.3, bf16[64,128]{1,0:T(8,128)(2,1)S(1)} %pack_row.1.own_ref.row_ref), custom_call_target="tpu_custom_call" | custom-call | tf_op jit(solution)/shard_map/pack_col/pallas_call | solution.py:125
  12.0 8.2 %all-to-all-start = ((bf16[16,32,128]{2,1,0:T(8,128)(2,1)}), bf16[16,32,128]{2,1,0:T(8,128)(2,1)S(1)}, u32[]{:S(2)}, u32[]{:S(2)}) async-start(bf16[16,32,128]{2,1,0:T(8,128)(2,1)} %pack_col.1), calls=%async_computation | async-start | bytes 262144 | tf_op jit(solution)/shard_map/all_to_all | solution.py:133
  20.3 0.0 collective-permute-done.first_ref
  20.3 6.1 %collective-permute-start.1 = (bf16[2,64,128]{2,1,0:T(8,128)(2,1)S(1)}, bf16[2,64,128]{2,1,0:T(8,128)(2,1)S(1)}, u32[]{:S(2)}, u32[]{:S(2)}) collective-permute-start(bf16[2,64,128]{2,1,0:T(8,128)(2,1)S(1)} %pad_maximum_fusion), channel_id=1, source_target_pairs={{0,96},{32,64},{64,32},{96,0},{1,97},{33,65},{65,33},{97,1},{2,98}... | collective-permute-start | bytes 98312 | tf_op jit(solution)/shard_map/ppermute | solution.py:136
  26.4 2.7 %collective-permute-done.1.other_ref = bf16[2,64,128]{2,1,0:T(8,128)(2,1)S(1)} collective-permute-done((bf16[2,64,128]{2,1,0:T(8,128)(2,1)S(1)}, bf16[2,64,128]{2,1,0:T(8,128)(2,1)S(1)}, u32[]{:S(2)}, u32[]{:S(2)}) %collective-permute-start.1) | collective-permute-done | bytes 32800 | tf_op jit(solution)/shard_map/ppermute | solution.py:136
  29.1 0.8 %fan.1 = bf16[4,4,64,128]{3,2,1,0:T(8,128)(2,1)} custom-call(bf16[64,128]{1,0:T(8,128)(2,1)S(1)} %pack_row.1.own_ref.row_ref, bf16[64,128]{1,0:T(8,128)(2,1)S(1)} %collective-permute-done.first_ref, bf16[2,64,128]{2,1,0:T(8,128)(2,1)S(1)} %collective-permute-done.1.other_ref), custom_call_target="tpu_custom_call" | custom-call | flops 4000000000 | bytes 262144 | tf_op jit(solution)/shard_map/fan/pallas_call | solution.py:137
  29.9 0.0 all-to-all-done.col_ref
  30.0 4.2 %all-to-all-start.1 = ((bf16[4,4,64,128]{3,2,1,0:T(8,128)(2,1)}), bf16[4,4,64,128]{3,2,1,0:T(8,128)(2,1)S(1)}, u32[]{:S(2)}, u32[]{:S(2)}) async-start(bf16[4,4,64,128]{3,2,1,0:T(8,128)(2,1)} %fan.1), calls=%async_computation.1 | async-start | bytes 524288 | tf_op jit(solution)/shard_map/all_to_all | solution.py:147
  34.1 3.2 %left.1 = (bf16[128,512]{1,0:T(8,128)(2,1)S(1)}, bf16[512,128]{1,0:T(8,128)(2,1)S(1)}, bf16[512,512]{1,0:T(8,128)(2,1)S(1)}, bf16[512,512]{1,0:T(8,128)(2,1)S(1)...) custom-call(bf16[16,32,128]{2,1,0:T(8,128)(2,1)S(1)} %all-to-all-done.col_ref, f32[512,512]{1,0:T(8,128)} %upper_ref.1, ...), custom_call_target="tpu_custom_call" | custom-call | tf_op jit(solution)/shard_map/left/pallas_call | solution.py:149
  37.3 2.3 %all-to-all-done.1 = bf16[4,4,64,128]{3,2,1,0:T(8,128)(2,1)S(1)} async-done(((bf16[4,4,64,128]{3,2,1,0:T(8,128)(2,1)}), bf16[4,4,64,128]{3,2,1,0:T(8,128)(2,1)S(1)}, u32[]{:S(2)}, u32[]{:S(2)}) %all-to-all-start.1) | async-done | bytes 262176 | tf_op jit(solution)/shard_map/all_to_all | solution.py:147
  39.7 5.3 %all-gather = bf16[8,4,64,128]{3,2,1,0:T(8,128)(2,1)S(1)} all-gather(bf16[4,4,64,128]{3,2,1,0:T(8,128)(2,1)S(1)} %all-to-all-done.1), channel_id=2, replica_groups=mesh['y'=4,'zh'=4,'core'=2,'zl'=4,'x'=4] {'core'}, dimensions={0}, use_global_device_ids=true | all-gather | bytes 786432 | tf_op jit(solution)/shard_map/all_gather | solution.py:148
  45.0 2.0 %schur.1 = bf16[512,2048]{1,0:T(8,128)(2,1)} custom-call(s32[1]{0:T(128)} %bitcast.me_ref, bf16[2,4,4,64,128]{4,3,2,1,0:T(8,128)(2,1)S(1)} %bitcast.4, bf16[128,512]{1,0:T(8,128)(2,1)S(1)} %get-tuple-element.15.q_ref, bf16[512,128]{1,0:T(8,128)(2,1)S(1)} %get-tuple-element.16.uu_ref, bf16[512,512]{1,0:T(8,128)(2,1)S(1)} %get-tuple-element.17.t0_ref, ...), custom_call_target="tpu_custom_call" | custom-call | tf_op jit(solution)/shard_map/schur/pallas_call | solution.py:161
  (1 shorter events, 0.0 us)
Async XLA Ops:
  0.8 19.4 %collective-permute-start = (bf16[64,128]{1,0:T(8,128)(2,1)S(1)}, bf16[64,128]{1,0:T(8,128)(2,1)S(1)}, u32[]{:S(2)}, u32[]{:S(2)}) collective-permute-start(bf16[64,128]{1,0:T(8,128)(2,1)S(1)} %pack_row.1.own_ref.row_ref), channel_id=1, source_target_pairs={{0,32},{32,0},{64,96},{96,64},{1,33},{33,1},{65,97},{97,65},{2,34}... | collective-permute-start | bytes 49160 | tf_op jit(solution)/shard_map/ppermute | solution.py:134
  12.0 17.9 %all-to-all-start = ((bf16[16,32,128]{2,1,0:T(8,128)(2,1)}), bf16[16,32,128]{2,1,0:T(8,128)(2,1)S(1)}, u32[]{:S(2)}, u32[]{:S(2)}) async-start(bf16[16,32,128]{2,1,0:T(8,128)(2,1)} %pack_col.1), calls=%async_computation | async-start | bytes 262144 | tf_op jit(solution)/shard_map/all_to_all | solution.py:133
  20.3 8.9 %collective-permute-start.1 = (bf16[2,64,128]{2,1,0:T(8,128)(2,1)S(1)}, bf16[2,64,128]{2,1,0:T(8,128)(2,1)S(1)}, u32[]{:S(2)}, u32[]{:S(2)}) collective-permute-start(bf16[2,64,128]{2,1,0:T(8,128)(2,1)S(1)} %pad_maximum_fusion), channel_id=1, source_target_pairs={{0,96},{32,64},{64,32},{96,0},{1,97},{33,65},{65,33},{97,1},{2,98}... | collective-permute-start | bytes 98312 | tf_op jit(solution)/shard_map/ppermute | solution.py:136
  30.0 9.7 %all-to-all-start.1 = ((bf16[4,4,64,128]{3,2,1,0:T(8,128)(2,1)}), bf16[4,4,64,128]{3,2,1,0:T(8,128)(2,1)S(1)}, u32[]{:S(2)}, u32[]{:S(2)}) async-start(bf16[4,4,64,128]{3,2,1,0:T(8,128)(2,1)} %fan.1), calls=%async_computation.1 | async-start | bytes 524288 | tf_op jit(solution)/shard_map/all_to_all | solution.py:147

commit v3 on v2

--- a/solution.py
+++ b/solution.py
@@ -20,16 +20,16 @@
     return lax.dot_general(a, b, (dims, ((), ())), preferred_element_type=F32)
 
 
-def pack_row_kernel(u_ref, v_ref, row_ref):
-    row_ref[:, :R] = u_ref[...].reshape(64, R)
-    row_ref[:, R:] = v_ref[...].reshape(64, R)
+def pack_kernel(ru_ref, rv_ref, cu_ref, cv_ref, row_ref, col_ref):
+    row_ref[:, :R] = ru_ref[...].reshape(64, R)
+    row_ref[:, R:] = rv_ref[...].reshape(64, R)
+    col_ref[:, :R] = cu_ref[0]
+    col_ref[:, R:] = cv_ref[0]
 
 
-def pack_col_kernel(u_ref, v_ref, row_ref, cols_hbm, buf, sem):
-    buf[:, :R] = u_ref[0]
-    buf[:, R:] = v_ref[0]
+def spread_kernel(col_ref, cols_hbm, sem):
     copies = [
-        pltpu.make_async_copy(buf, cols_hbm.at[k], sem.at[k]) for k in range(ZL * X)
+        pltpu.make_async_copy(col_ref, cols_hbm.at[k], sem.at[k]) for k in range(ZL * X)
     ]
     for c in copies:
         c.start()
@@ -115,21 +115,21 @@
 def shards(trailing, col_u, col_v, row_u, row_v, diag_lower_inv, diag_upper_inv):
     vmem = pl.BlockSpec(memory_space=pltpu.VMEM)
     hbm = pl.BlockSpec(memory_space=pl.ANY)
-    row = pl.pallas_call(
-        pack_row_kernel,
-        in_specs=[vmem] * 2,
-        out_specs=vmem,
-        out_shape=pltpu.VMEM((64, 128), BF16),
-        name="pack_row",
-    )(row_u, row_v)
+    row, col = pl.pallas_call(
+        pack_kernel,
+        in_specs=[vmem] * 4,
+        out_specs=(vmem, vmem),
+        out_shape=(pltpu.VMEM((64, 128), BF16), pltpu.VMEM((32, 128), BF16)),
+        name="pack",
+    )(row_u, row_v, col_u, col_v)
     col_sends = pl.pallas_call(
-        pack_col_kernel,
-        in_specs=[vmem] * 3,
+        spread_kernel,
+        in_specs=[vmem],
         out_specs=hbm,
         out_shape=pltpu.HBM((ZL * X, 32, 128), BF16),
-        scratch_shapes=[pltpu.VMEM((32, 128), BF16), pltpu.SemaphoreType.DMA((ZL * X,))],
-        name="pack_col",
-    )(col_u, col_v, *on_chip(row))
+        scratch_shapes=[pltpu.SemaphoreType.DMA((ZL * X,))],
+        name="spread",
+    )(*on_chip(col))
     cols = lax.all_to_all(col_sends, COL, 0, 0, tiled=True)
     first = lax.ppermute(row, "zh", [(k, k ^ 1) for k in range(ZH)])
     pair = jnp.stack([first, row])

time: 47.6 us -> 46.7 us (0.981)
  Pallas kernels: 8.41 us -> 7.63 us
    pallas_call x2, Pallas kernels: 2.39 us -> 1.62 us  [the longest x1 0.82 us: shards(): pl.pallas_call(pack_kernel, in_specs=[vmem] * 4, out_specs=(vmem, vmem),...]
  transfers between devices with their start and end apart: 4 -> 4, of which waited for: 2 -> 2; matrix products, arithmetic and copies ran while one was open for 0% -> 0% of each run, Pallas kernels for 12% -> 10%
where the time goes in v3:
time: 46.7 us; the launch traced here: 46.3 us
  starting transfers between devices  28.2 us (60%)
  Pallas kernels  7.63 us (16%)
  blocking collectives  5.32 us (11%)
  waiting for transfers between devices  5.08 us (11%)
    ppermute x1, starting transfers between devices, shards(): first = lax.ppermute(row, 'zh', [(k, k ^ 1) for k in range(ZH)])  9.64 us
    all_to_all x1, starting transfers between devices, shards(): cols = lax.all_to_all(col_sends, COL, 0, 0, tiled=True)  8.2 us
    ppermute x1, starting transfers between devices, shards(): other = lax.ppermute(pair, 'zh', [(k, k ^ 3) for k in range(ZH)])  6.12 us
    all_gather x1, blocking collectives, shards(): everything = lax.all_gather(over_y, 'core', axis=0, tiled=False)  5.32 us
    all_to_all x1, starting transfers between devices, shards(): over_y = lax.all_to_all(sends, 'y', 0, 0, tiled=True)  4.2 us
    pallas_call x1, Pallas kernels, shards(): pl.pallas_call(left_kernel, in_specs=[vmem] * 3 + [hbm], out_specs=(vmem,...  3.18 us
    ppermute x1, waiting for transfers between devices, shards(): other = lax.ppermute(pair, 'zh', [(k, k ^ 3) for k in range(ZH)])  2.73 us
    all_to_all x1, waiting for transfers between devices, shards(): over_y = lax.all_to_all(sends, 'y', 0, 0, tiled=True)  2.34 us
  transfers between devices with their start and end apart: 4, of which 2 were waited for; matrix products, arithmetic and copies ran while one was open for 0% of the time, Pallas kernels for 10%

profile of v3, /device:TPU:1, one launch (start us, length us, event | category | flops | bytes accessed | tf_op | source)
XLA Modules:
  0.0 46.3 jit_solution(4146020628892906870)
XLA Ops:
  0.0 0.8 %pack.1 = (bf16[64,128]{1,0:T(8,128)(2,1)S(1)}, bf16[32,128]{1,0:T(8,128)(2,1)S(1)}) custom-call(bf16[4,16,64]{2,1,0:T(8,128)(2,1)} %ru_ref.1, bf16[4,16,64]{2,1,0:T(8,128)(2,1)} %rv_ref.1, bf16[1,32,64]{2,1,0:T(8,128)(2,1)} %cu_ref.1, bf16[1,32,64]{2,1,0:T(8,128)(2,1)} %cv_ref.1), custom_call_target="tpu_custom_call" | custom-call | tf_op jit(solution)/shard_map/pack/pallas_call | solution.py:118
  0.8 9.6 %collective-permute-start = (bf16[64,128]{1,0:T(8,128)(2,1)S(1)}, bf16[64,128]{1,0:T(8,128)(2,1)S(1)}, u32[]{:S(2)}, u32[]{:S(2)}) collective-permute-start(bf16[64,128]{1,0:T(8,128)(2,1)S(1)} %get-tuple-element.15.own_ref), channel_id=1, source_target_pairs={{0,32},{32,0},{64,96},{96,64},{1,33},{33,1},{65,97},{97,65},{2,34}... | collective-permute-start | bytes 49160 | tf_op jit(solution)/shard_map/ppermute | solution.py:134
  10.5 0.8 %spread.1 = bf16[16,32,128]{2,1,0:T(8,128)(2,1)} custom-call(bf16[32,128]{1,0:T(8,128)(2,1)S(1)} %get-tuple-element.16.col_ref), custom_call_target="tpu_custom_call" | custom-call | tf_op jit(solution)/shard_map/spread/pallas_call | solution.py:125
  11.3 8.2 %all-to-all-start = ((bf16[16,32,128]{2,1,0:T(8,128)(2,1)}), bf16[16,32,128]{2,1,0:T(8,128)(2,1)S(1)}, u32[]{:S(2)}, u32[]{:S(2)}) async-start(bf16[16,32,128]{2,1,0:T(8,128)(2,1)} %spread.1), calls=%async_computation | async-start | bytes 262144 | tf_op jit(solution)/shard_map/all_to_all | solution.py:133
  19.5 0.0 collective-permute-done.first_ref
  19.5 6.1 %collective-permute-start.1 = (bf16[2,64,128]{2,1,0:T(8,128)(2,1)S(1)}, bf16[2,64,128]{2,1,0:T(8,128)(2,1)S(1)}, u32[]{:S(2)}, u32[]{:S(2)}) collective-permute-start(bf16[2,64,128]{2,1,0:T(8,128)(2,1)S(1)} %pad_maximum_fusion), channel_id=1, source_target_pairs={{0,96},{32,64},{64,32},{96,0},{1,97},{33,65},{65,33},{97,1},{2,98}... | collective-permute-start | bytes 98312 | tf_op jit(solution)/shard_map/ppermute | solution.py:136
  25.6 2.7 %collective-permute-done.1.other_ref = bf16[2,64,128]{2,1,0:T(8,128)(2,1)S(1)} collective-permute-done((bf16[2,64,128]{2,1,0:T(8,128)(2,1)S(1)}, bf16[2,64,128]{2,1,0:T(8,128)(2,1)S(1)}, u32[]{:S(2)}, u32[]{:S(2)}) %collective-permute-start.1) | collective-permute-done | bytes 32800 | tf_op jit(solution)/shard_map/ppermute | solution.py:136
  28.4 0.8 %fan.1 = bf16[4,4,64,128]{3,2,1,0:T(8,128)(2,1)} custom-call(bf16[64,128]{1,0:T(8,128)(2,1)S(1)} %get-tuple-element.15.own_ref, bf16[64,128]{1,0:T(8,128)(2,1)S(1)} %collective-permute-done.first_ref, bf16[2,64,128]{2,1,0:T(8,128)(2,1)S(1)} %collective-permute-done.1.other_ref), custom_call_target="tpu_custom_call" | custom-call | flops 4000000000 | bytes 262144 | tf_op jit(solution)/shard_map/fan/pallas_call | solution.py:137
  29.2 0.0 all-to-all-done.col_ref
  29.2 4.2 %all-to-all-start.1 = ((bf16[4,4,64,128]{3,2,1,0:T(8,128)(2,1)}), bf16[4,4,64,128]{3,2,1,0:T(8,128)(2,1)S(1)}, u32[]{:S(2)}, u32[]{:S(2)}) async-start(bf16[4,4,64,128]{3,2,1,0:T(8,128)(2,1)} %fan.1), calls=%async_computation.1 | async-start | bytes 524288 | tf_op jit(solution)/shard_map/all_to_all | solution.py:147
  33.4 3.2 %left.1 = (bf16[128,512]{1,0:T(8,128)(2,1)S(1)}, bf16[512,128]{1,0:T(8,128)(2,1)S(1)}, bf16[512,512]{1,0:T(8,128)(2,1)S(1)}, bf16[512,512]{1,0:T(8,128)(2,1)S(1)...) custom-call(bf16[16,32,128]{2,1,0:T(8,128)(2,1)S(1)} %all-to-all-done.col_ref, f32[512,512]{1,0:T(8,128)} %upper_ref.1, ...), custom_call_target="tpu_custom_call" | custom-call | tf_op jit(solution)/shard_map/left/pallas_call | solution.py:149
  36.6 2.3 %all-to-all-done.1 = bf16[4,4,64,128]{3,2,1,0:T(8,128)(2,1)S(1)} async-done(((bf16[4,4,64,128]{3,2,1,0:T(8,128)(2,1)}), bf16[4,4,64,128]{3,2,1,0:T(8,128)(2,1)S(1)}, u32[]{:S(2)}, u32[]{:S(2)}) %all-to-all-start.1) | async-done | bytes 262176 | tf_op jit(solution)/shard_map/all_to_all | solution.py:147
  38.9 5.3 %all-gather = bf16[8,4,64,128]{3,2,1,0:T(8,128)(2,1)S(1)} all-gather(bf16[4,4,64,128]{3,2,1,0:T(8,128)(2,1)S(1)} %all-to-all-done.1), channel_id=2, replica_groups=mesh['y'=4,'zh'=4,'core'=2,'zl'=4,'x'=4] {'core'}, dimensions={0}, use_global_device_ids=true | all-gather | bytes 786432 | tf_op jit(solution)/shard_map/all_gather | solution.py:148
  44.2 2.0 %schur.1 = bf16[512,2048]{1,0:T(8,128)(2,1)} custom-call(s32[1]{0:T(128)} %bitcast.me_ref, bf16[2,4,4,64,128]{4,3,2,1,0:T(8,128)(2,1)S(1)} %bitcast.4, bf16[128,512]{1,0:T(8,128)(2,1)S(1)} %get-tuple-element.19.q_ref, bf16[512,128]{1,0:T(8,128)(2,1)S(1)} %get-tuple-element.20.uu_ref, bf16[512,512]{1,0:T(8,128)(2,1)S(1)} %get-tuple-element.21.t0_ref, ...), custom_call_target="tpu_custom_call" | custom-call | tf_op jit(solution)/shard_map/schur/pallas_call | solution.py:161
  (1 shorter events, 0.0 us)
Async XLA Ops:
  0.8 18.7 %collective-permute-start = (bf16[64,128]{1,0:T(8,128)(2,1)S(1)}, bf16[64,128]{1,0:T(8,128)(2,1)S(1)}, u32[]{:S(2)}, u32[]{:S(2)}) collective-permute-start(bf16[64,128]{1,0:T(8,128)(2,1)S(1)} %get-tuple-element.15.own_ref), channel_id=1, source_target_pairs={{0,32},{32,0},{64,96},{96,64},{1,33},{33,1},{65,97},{97,65},{2,34}... | collective-permute-start | bytes 49160 | tf_op jit(solution)/shard_map/ppermute | solution.py:134
  11.3 17.9 %all-to-all-start = ((bf16[16,32,128]{2,1,0:T(8,128)(2,1)}), bf16[16,32,128]{2,1,0:T(8,128)(2,1)S(1)}, u32[]{:S(2)}, u32[]{:S(2)}) async-start(bf16[16,32,128]{2,1,0:T(8,128)(2,1)} %spread.1), calls=%async_computation | async-start | bytes 262144 | tf_op jit(solution)/shard_map/all_to_all | solution.py:133
  19.5 8.9 %collective-permute-start.1 = (bf16[2,64,128]{2,1,0:T(8,128)(2,1)S(1)}, bf16[2,64,128]{2,1,0:T(8,128)(2,1)S(1)}, u32[]{:S(2)}, u32[]{:S(2)}) collective-permute-start(bf16[2,64,128]{2,1,0:T(8,128)(2,1)S(1)} %pad_maximum_fusion), channel_id=1, source_target_pairs={{0,96},{32,64},{64,32},{96,0},{1,97},{33,65},{65,33},{97,1},{2,98}... | collective-permute-start | bytes 98312 | tf_op jit(solution)/shard_map/ppermute | solution.py:136
  29.2 9.7 %all-to-all-start.1 = ((bf16[4,4,64,128]{3,2,1,0:T(8,128)(2,1)}), bf16[4,4,64,128]{3,2,1,0:T(8,128)(2,1)S(1)}, u32[]{:S(2)}, u32[]{:S(2)}) async-start(bf16[4,4,64,128]{3,2,1,0:T(8,128)(2,1)} %fan.1), calls=%async_computation.1 | async-start | bytes 524288 | tf_op jit(solution)/shard_map/all_to_all | solution.py:147

commit v4 on v3

--- a/solution.py
+++ b/solution.py
@@ -5,8 +5,10 @@
 from jax.experimental.pallas import tpu as pltpu
 from jax.sharding import Mesh, PartitionSpec as P
 
-Y, ZH, CORE, ZL, X = 4, 4, 2, 4, 4
-ROW, COL = ("y", "zh", "core"), ("zl", "x")
+Y, ZH, CORE, C = 4, 4, 2, 16
+ROW, COL = ("y", "zh", "core"), ("c",)
+Y_ORDER = [2, 3, 0, 1]
+C_ORDER = list(range(C))
 B, R = 512, 64
 F32, BF16 = jnp.float32, jnp.bfloat16
 
@@ -29,7 +31,7 @@
 
 def spread_kernel(col_ref, cols_hbm, sem):
     copies = [
-        pltpu.make_async_copy(col_ref, cols_hbm.at[k], sem.at[k]) for k in range(ZL * X)
+        pltpu.make_async_copy(col_ref, cols_hbm.at[k], sem.at[k]) for k in range(C)
     ]
     for c in copies:
         c.start()
@@ -52,7 +54,7 @@
         c.wait()
 
 
-def left_kernel(col_ref, upper_ref, lower_ref, t_hbm, q_ref, uu_ref, *rest):
+def fetch_kernel(after_ref, t_hbm, *rest):
     held, sem = rest[:-1], rest[-1]
     fetch = [
         pltpu.make_async_copy(t_hbm.at[:, pl.ds(j * B, B)], h, sem.at[j])
@@ -60,7 +62,12 @@
     ]
     for f in fetch:
         f.start()
-    col = col_ref[...].reshape(B, 2 * R)
+    for f in fetch:
+        f.wait()
+
+
+def left_kernel(col_ref, upper_ref, lower_ref, q_ref, uu_ref):
+    col = jnp.concatenate([col_ref[C_ORDER.index(c)] for c in range(C)], axis=0)
     u = col[:, :R]
     uu_ref[:, :R] = u
     uu_ref[:, R:] = u
@@ -74,8 +81,6 @@
     q_hi, q_lo = split(q)
     q_ref[:R] = q_hi
     q_ref[R:] = q_lo
-    for f in fetch:
-        f.wait()
 
 
 def schur_kernel(me_ref, x_ref, q_ref, uu_ref, t0_ref, t1_ref, t2_ref, t3_ref, o_hbm, obuf, osem):
@@ -85,7 +90,7 @@
     slot = [me ^ z for z in range(ZH)]
     order = [(c, y, z) for y in range(Y) for z in range(ZH) for c in range(CORE)]
     xs = [
-        jnp.concatenate([x_ref[c, y, slot[z], j * 16 : (j + 1) * 16, :] for c, y, z in order], axis=0)
+        jnp.concatenate([x_ref[c, Y_ORDER.index(y), slot[z], j * 16 : (j + 1) * 16, :] for c, y, z in order], axis=0)
         for j in range(tiles)
     ]
     q = q_ref[...]
@@ -112,6 +117,13 @@
     return tuple(pltpu.with_memory_space_constraint(a, pltpu.VMEM) for a in arrays)
 
 
+def off_chip(*arrays):
+    return tuple(pltpu.with_memory_space_constraint(a, pltpu.HBM) for a in arrays)
+
+
+SMALL = pltpu.CompilerParams(vmem_limit_bytes=16 << 20)
+
+
 def shards(trailing, col_u, col_v, row_u, row_v, diag_lower_inv, diag_upper_inv):
     vmem = pl.BlockSpec(memory_space=pltpu.VMEM)
     hbm = pl.BlockSpec(memory_space=pl.ANY)
@@ -126,38 +138,47 @@
         spread_kernel,
         in_specs=[vmem],
         out_specs=hbm,
-        out_shape=pltpu.HBM((ZL * X, 32, 128), BF16),
-        scratch_shapes=[pltpu.SemaphoreType.DMA((ZL * X,))],
+        out_shape=pltpu.HBM((C, 32, 128), BF16),
+        scratch_shapes=[pltpu.SemaphoreType.DMA((C,))],
         name="spread",
     )(*on_chip(col))
-    cols = lax.all_to_all(col_sends, COL, 0, 0, tiled=True)
+    cols = lax.all_to_all(
+        col_sends, "c", 0, 0, tiled=True, axis_index_groups=[C_ORDER]
+    )
     first = lax.ppermute(row, "zh", [(k, k ^ 1) for k in range(ZH)])
     pair = jnp.stack([first, row])
     other = lax.ppermute(pair, "zh", [(k, k ^ 3) for k in range(ZH)])
+    held = pl.pallas_call(
+        fetch_kernel,
+        in_specs=[vmem, hbm],
+        out_specs=(vmem,) * 4,
+        out_shape=(pltpu.VMEM((B, B), BF16),) * 4,
+        scratch_shapes=[pltpu.SemaphoreType.DMA((4,))],
+        compiler_params=SMALL,
+        name="fetch",
+    )(*on_chip(pair), *off_chip(trailing))
+    other, held = lax.optimization_barrier((other, held))
     sends = pl.pallas_call(
         fan_kernel,
         in_specs=[vmem] * 3,
         out_specs=hbm,
         out_shape=pltpu.HBM((Y, ZH, 64, 128), BF16),
         scratch_shapes=[pltpu.SemaphoreType.DMA((Y, 3))],
-        cost_estimate=pl.CostEstimate(flops=4_000_000_000, transcendentals=0, bytes_accessed=1 << 18),
+        cost_estimate=pl.CostEstimate(flops=4000000000, transcendentals=0, bytes_accessed=1 << 18),
+        compiler_params=SMALL,
         name="fan",
     )(*on_chip(row, first, other))
     sends, cols = lax.optimization_barrier((sends, cols))
-    over_y = lax.all_to_all(sends, "y", 0, 0, tiled=True)
+    over_y = lax.all_to_all(sends, "y", 0, 0, tiled=True, axis_index_groups=[Y_ORDER])
     everything = lax.all_gather(over_y, "core", axis=0, tiled=False)
-    q, uu, *held = pl.pallas_call(
+    q, uu = pl.pallas_call(
         left_kernel,
-        in_specs=[vmem] * 3 + [hbm],
-        out_specs=(vmem,) * 6,
-        out_shape=(
-            pltpu.VMEM((2 * R, B), BF16),
-            pltpu.VMEM((B, 2 * R), BF16),
-            *[pltpu.VMEM((B, B), BF16)] * 4,
-        ),
-        scratch_shapes=[pltpu.SemaphoreType.DMA((4,))],
+        in_specs=[vmem] * 3,
+        out_specs=(vmem, vmem),
+        out_shape=(pltpu.VMEM((2 * R, B), BF16), pltpu.VMEM((B, 2 * R), BF16)),
+        compiler_params=SMALL,
         name="left",
-    )(*on_chip(cols), diag_upper_inv, diag_lower_inv, trailing)
+    )(*on_chip(cols), *off_chip(diag_upper_inv, diag_lower_inv))
     return pl.pallas_call(
         schur_kernel,
         in_specs=[pl.BlockSpec(memory_space=pltpu.SMEM)] + [vmem] * 7,
@@ -172,7 +193,7 @@
 
 
 def solution(mesh):
-    parts = Mesh(mesh.devices.reshape(Y, ZH, CORE, ZL, X), ROW + COL)
+    parts = Mesh(mesh.devices.reshape(Y, ZH, CORE, C), ROW + COL)
     placed = (
         P(ROW, COL),
         P(ROW, COL, None),

time: 46.7 us -> 45.8 us (0.981)
  waiting for transfers between devices: 5.08 us -> 1.69 us
  starting transfers between devices: 28.2 us -> 30.3 us
  Pallas kernels: 7.63 us -> 8.34 us
    all_to_all x2, starting transfers between devices: 12.4 us -> 14.5 us  [the longest x1 8.2 us: shards(): lax.all_to_all(col_sends, 'c', 0, 0, tiled=True, axis_index_groups=[C_ORD...]
    all_to_all x2, waiting for transfers between devices: 2.35 us -> 0.53 us  [the longest x1 0.53 us: shards(): lax.all_to_all(sends, 'y', 0, 0, tiled=True, axis_index_groups=[Y_ORDER])]
    ppermute x1, waiting for transfers between devices: 2.73 us -> 1.16 us  [shards(): other = lax.ppermute(pair, 'zh', [(k, k ^ 3) for k in range(ZH)])]
    pallas_call x1 -> x2, Pallas kernels: 3.18 us -> 3.87 us  [the longest x1 2.31 us: shards(): pl.pallas_call(left_kernel, in_specs=[vmem] * 3, out_specs=(vmem, vmem),...]
  transfers between devices with their start and end apart: 4 -> 4, of which waited for: 2 -> 2; matrix products, arithmetic and copies ran while one was open for 0% -> 0% of each run, Pallas kernels for 10% -> 12%
where the time goes in v4:
time: 45.8 us; the launch traced here: 45.4 us
  starting transfers between devices  30.3 us (66%)
  Pallas kernels  8.34 us (18%)
  blocking collectives  5.04 us (11%)
  waiting for transfers between devices  1.69 us (4%)
    ppermute x1, starting transfers between devices, shards(): first = lax.ppermute(row, 'zh', [(k, k ^ 1) for k in range(ZH)])  9.64 us
    all_to_all x1, starting transfers between devices, shards(): lax.all_to_all(col_sends, 'c', 0, 0, tiled=True, axis_index_groups=[C_ORD...  8.2 us
    all_to_all x1, starting transfers between devices, shards(): lax.all_to_all(sends, 'y', 0, 0, tiled=True, axis_index_groups=[Y_ORDER])  6.3 us
    ppermute x1, starting transfers between devices, shards(): other = lax.ppermute(pair, 'zh', [(k, k ^ 3) for k in range(ZH)])  6.12 us
    all_gather x1, blocking collectives, shards(): everything = lax.all_gather(over_y, 'core', axis=0, tiled=False)  5.04 us
    pallas_call x1, Pallas kernels, shards(): pl.pallas_call(left_kernel, in_specs=[vmem] * 3, out_specs=(vmem, vmem),...  2.31 us
    pallas_call x1, Pallas kernels, shards(): pl.pallas_call(schur_kernel, in_specs=[pl.BlockSpec(memory_space=pltpu.SM...  2.04 us
    pallas_call x1, Pallas kernels, shards(): pl.pallas_call(fetch_kernel, in_specs=[vmem, hbm], out_specs=(vmem,) * 4,...  1.57 us
  transfers between devices with their start and end apart: 4, of which 2 were waited for; matrix products, arithmetic and copies ran while one was open for 0% of the time, Pallas kernels for 12%

profile of v4, /device:TPU:1, one launch (start us, length us, event | category | flops | bytes accessed | tf_op | source)
XLA Modules:
  0.0 45.4 jit_solution(5875442749364513575)
XLA Ops:
  0.0 0.8 %pack.1 = (bf16[64,128]{1,0:T(8,128)(2,1)S(1)}, bf16[32,128]{1,0:T(8,128)(2,1)S(1)}) custom-call(bf16[4,16,64]{2,1,0:T(8,128)(2,1)} %ru_ref.1, bf16[4,16,64]{2,1,0:T(8,128)(2,1)} %rv_ref.1, bf16[1,32,64]{2,1,0:T(8,128)(2,1)} %cu_ref.1, bf16[1,32,64]{2,1,0:T(8,128)(2,1)} %cv_ref.1), custom_call_target="tpu_custom_call" | custom-call | tf_op jit(solution)/shard_map/pack/pallas_call | solution.py:130
  0.8 9.6 %collective-permute-start = (bf16[64,128]{1,0:T(8,128)(2,1)S(1)}, bf16[64,128]{1,0:T(8,128)(2,1)S(1)}, u32[]{:S(2)}, u32[]{:S(2)}) collective-permute-start(bf16[64,128]{1,0:T(8,128)(2,1)S(1)} %get-tuple-element.20.own_ref), channel_id=1, source_target_pairs={{0,32},{32,0},{64,96},{96,64},{1,33},{33,1},{65,97},{97,65},{2,34}... | collective-permute-start | bytes 49160 | tf_op jit(solution)/shard_map/ppermute | solution.py:148
  10.5 0.8 %spread.1 = bf16[16,32,128]{2,1,0:T(8,128)(2,1)} custom-call(bf16[32,128]{1,0:T(8,128)(2,1)S(1)} %get-tuple-element.26.col_ref), custom_call_target="tpu_custom_call" | custom-call | tf_op jit(solution)/shard_map/spread/pallas_call | solution.py:137
  11.3 8.2 %all-to-all-start = ((bf16[16,32,128]{2,1,0:T(8,128)(2,1)}), bf16[16,32,128]{2,1,0:T(8,128)(2,1)S(1)}, u32[]{:S(2)}, u32[]{:S(2)}) async-start(bf16[16,32,128]{2,1,0:T(8,128)(2,1)} %spread.1), calls=%async_computation | async-start | bytes 262144 | tf_op jit(solution)/shard_map/all_to_all | solution.py:145
  19.5 0.0 collective-permute-done.first_ref
  19.5 6.1 %collective-permute-start.1 = (bf16[2,64,128]{2,1,0:T(8,128)(2,1)S(1)}, bf16[2,64,128]{2,1,0:T(8,128)(2,1)S(1)}, u32[]{:S(2)}, u32[]{:S(2)}) collective-permute-start(bf16[2,64,128]{2,1,0:T(8,128)(2,1)S(1)} %pad_maximum_fusion.after_ref), channel_id=1, source_target_pairs={{0,96},{32,64},{64,32},{96,0},{1,97},{33,65},{65,33},{97,1},{2,98}... | collective-permute-start | bytes 98312 | tf_op jit(solution)/shard_map/ppermute | solution.py:150
  25.6 1.6 %fetch.1 = (bf16[512,512]{1,0:T(8,128)(2,1)S(1)}, bf16[512,512]{1,0:T(8,128)(2,1)S(1)}, bf16[512,512]{1,0:T(8,128)(2,1)S(1)}, bf16[512,512]{1,0:T(8,128)(2,1)S(1)}) custom-call(bf16[2,64,128]{2,1,0:T(8,128)(2,1)S(1)} %pad_maximum_fusion.after_ref, bf16[512,2048]{1,0:T(8,128)(2,1)} %t_hbm.1), custom_call_target="tpu_custom_call" | custom-call | tf_op jit(solution)/shard_map/fetch/pallas_call | solution.py:151
  27.2 1.2 %collective-permute-done.1.other_ref = bf16[2,64,128]{2,1,0:T(8,128)(2,1)S(1)} collective-permute-done((bf16[2,64,128]{2,1,0:T(8,128)(2,1)S(1)}, bf16[2,64,128]{2,1,0:T(8,128)(2,1)S(1)}, u32[]{:S(2)}, u32[]{:S(2)}) %collective-permute-start.1) | collective-permute-done | bytes 32800 | tf_op jit(solution)/shard_map/ppermute | solution.py:150
  28.4 0.8 %fan.1 = bf16[4,4,64,128]{3,2,1,0:T(8,128)(2,1)} custom-call(bf16[64,128]{1,0:T(8,128)(2,1)S(1)} %get-tuple-element.20.own_ref, bf16[64,128]{1,0:T(8,128)(2,1)S(1)} %collective-permute-done.first_ref, bf16[2,64,128]{2,1,0:T(8,128)(2,1)S(1)} %collective-permute-done.1.other_ref), custom_call_target="tpu_custom_call" | custom-call | flops 4000000000 | bytes 262144 | tf_op jit(solution)/shard_map/fan/pallas_call | solution.py:161
  29.2 0.0 all-to-all-done.col_ref
  29.2 6.3 %all-to-all-start.1 = ((bf16[4,4,64,128]{3,2,1,0:T(8,128)(2,1)}), bf16[4,4,64,128]{3,2,1,0:T(8,128)(2,1)S(1)}, u32[]{:S(2)}, u32[]{:S(2)}) async-start(bf16[4,4,64,128]{3,2,1,0:T(8,128)(2,1)} %fan.1), calls=%async_computation.1 | async-start | bytes 524288 | tf_op jit(solution)/shard_map/all_to_all | solution.py:172
  35.5 2.3 %left.1 = (bf16[128,512]{1,0:T(8,128)(2,1)S(1)}, bf16[512,128]{1,0:T(8,128)(2,1)S(1)}) custom-call(bf16[16,32,128]{2,1,0:T(8,128)(2,1)S(1)} %all-to-all-done.col_ref, f32[512,512]{1,0:T(8,128)} %upper_ref.1, f32[512,512]{1,0:T(8,128)} %lower_ref.1), custom_call_target="tpu_custom_call" | custom-call | tf_op jit(solution)/shard_map/left/pallas_call | solution.py:174
  37.8 0.5 %all-to-all-done.1 = bf16[4,4,64,128]{3,2,1,0:T(8,128)(2,1)S(1)} async-done(((bf16[4,4,64,128]{3,2,1,0:T(8,128)(2,1)}), bf16[4,4,64,128]{3,2,1,0:T(8,128)(2,1)S(1)}, u32[]{:S(2)}, u32[]{:S(2)}) %all-to-all-start.1) | async-done | bytes 262176 | tf_op jit(solution)/shard_map/all_to_all | solution.py:172
  38.3 5.0 %all-gather = bf16[8,4,64,128]{3,2,1,0:T(8,128)(2,1)S(1)} all-gather(bf16[4,4,64,128]{3,2,1,0:T(8,128)(2,1)S(1)} %all-to-all-done.1), channel_id=2, replica_groups=mesh['y'=4,'zh'=4,'core'=2,'c'=16] {'core'}, dimensions={0}, use_global_device_ids=true | all-gather | bytes 786432 | tf_op jit(solution)/shard_map/all_gather | solution.py:173
  43.4 2.0 %schur.1 = bf16[512,2048]{1,0:T(8,128)(2,1)} custom-call(s32[1]{0:T(128)} %bitcast.me_ref, bf16[2,4,4,64,128]{4,3,2,1,0:T(8,128)(2,1)S(1)} %bitcast.4, bf16[128,512]{1,0:T(8,128)(2,1)S(1)} %get-tuple-element.29.q_ref, bf16[512,128]{1,0:T(8,128)(2,1)S(1)} %get-tuple-element.30.uu_ref, bf16[512,512]{1,0:T(8,128)(2,1)S(1)} %get-tuple-element.31.t0_ref, ...), custom_call_target="tpu_custom_call" | custom-call | tf_op jit(solution)/shard_map/schur/pallas_call | solution.py:182
  (1 shorter events, 0.0 us)
Async XLA Ops:
  0.8 18.7 %collective-permute-start = (bf16[64,128]{1,0:T(8,128)(2,1)S(1)}, bf16[64,128]{1,0:T(8,128)(2,1)S(1)}, u32[]{:S(2)}, u32[]{:S(2)}) collective-permute-start(bf16[64,128]{1,0:T(8,128)(2,1)S(1)} %get-tuple-element.20.own_ref), channel_id=1, source_target_pairs={{0,32},{32,0},{64,96},{96,64},{1,33},{33,1},{65,97},{97,65},{2,34}... | collective-permute-start | bytes 49160 | tf_op jit(solution)/shard_map/ppermute | solution.py:148
  11.3 17.9 %all-to-all-start = ((bf16[16,32,128]{2,1,0:T(8,128)(2,1)}), bf16[16,32,128]{2,1,0:T(8,128)(2,1)S(1)}, u32[]{:S(2)}, u32[]{:S(2)}) async-start(bf16[16,32,128]{2,1,0:T(8,128)(2,1)} %spread.1), calls=%async_computation | async-start | bytes 262144 | tf_op jit(solution)/shard_map/all_to_all | solution.py:145
  19.5 8.9 %collective-permute-start.1 = (bf16[2,64,128]{2,1,0:T(8,128)(2,1)S(1)}, bf16[2,64,128]{2,1,0:T(8,128)(2,1)S(1)}, u32[]{:S(2)}, u32[]{:S(2)}) collective-permute-start(bf16[2,64,128]{2,1,0:T(8,128)(2,1)S(1)} %pad_maximum_fusion.after_ref), channel_id=1, source_target_pairs={{0,96},{32,64},{64,32},{96,0},{1,97},{33,65},{65,33},{97,1},{2,98}... | collective-permute-start | bytes 98312 | tf_op jit(solution)/shard_map/ppermute | solution.py:150
  29.2 9.1 %all-to-all-start.1 = ((bf16[4,4,64,128]{3,2,1,0:T(8,128)(2,1)}), bf16[4,4,64,128]{3,2,1,0:T(8,128)(2,1)S(1)}, u32[]{:S(2)}, u32[]{:S(2)}) async-start(bf16[4,4,64,128]{3,2,1,0:T(8,128)(2,1)} %fan.1), calls=%async_computation.1 | async-start | bytes 524288 | tf_op jit(solution)/shard_map/all_to_all | solution.py:172

commit v5 on v4

--- a/solution.py
+++ b/solution.py
@@ -8,7 +8,7 @@
 Y, ZH, CORE, C = 4, 4, 2, 16
 ROW, COL = ("y", "zh", "core"), ("c",)
 Y_ORDER = [2, 3, 0, 1]
-C_ORDER = list(range(C))
+C_ORDER = [4, *[c for c in range(C) if c != 4]]
 B, R = 512, 64
 F32, BF16 = jnp.float32, jnp.bfloat16
 
@@ -20,6 +20,11 @@
 
 def dot(a, b, dims=((1,), (0,))):
     return lax.dot_general(a, b, (dims, ((), ())), preferred_element_type=F32)
+
+
+def crossed(array, bits):
+    swap = [(2 * k + c, 2 * (k ^ bits) + 1 - c) for k in range(ZH) for c in range(CORE)]
+    return lax.ppermute(array, ("zh", "core"), swap)
 
 
 def pack_kernel(ru_ref, rv_ref, cu_ref, cv_ref, row_ref, col_ref):
@@ -90,7 +95,7 @@
     slot = [me ^ z for z in range(ZH)]
     order = [(c, y, z) for y in range(Y) for z in range(ZH) for c in range(CORE)]
     xs = [
-        jnp.concatenate([x_ref[c, Y_ORDER.index(y), slot[z], j * 16 : (j + 1) * 16, :] for c, y, z in order], axis=0)
+        jnp.concatenate([x_ref[c ^ (slot[z] >> 1), Y_ORDER.index(y), slot[z], j * 16 : (j + 1) * 16, :] for c, y, z in order], axis=0)
         for j in range(tiles)
     ]
     q = q_ref[...]
@@ -147,7 +152,7 @@
     )
     first = lax.ppermute(row, "zh", [(k, k ^ 1) for k in range(ZH)])
     pair = jnp.stack([first, row])
-    other = lax.ppermute(pair, "zh", [(k, k ^ 3) for k in range(ZH)])
+    other = crossed(pair, 3)
     held = pl.pallas_call(
         fetch_kernel,
         in_specs=[vmem, hbm],

time: 45.8 us -> 45.8 us (level)
  starting transfers between devices: 30.3 us -> 31.8 us
  waiting for transfers between devices: 1.69 us -> 0.69 us
  blocking collectives: 5.04 us -> 4.4 us
    ppermute x1, starting transfers between devices: 6.12 us -> 7.52 us  [crossed(): return lax.ppermute(array, ('zh', 'core'), swap)]
    ppermute x1, waiting for transfers between devices: 1.16 us -> 0.15 us  [crossed(): return lax.ppermute(array, ('zh', 'core'), swap)]
    all_gather x1, blocking collectives: 5.04 us -> 4.4 us  [shards(): everything = lax.all_gather(over_y, 'core', axis=0, tiled=False)]
where the time goes in v5:
time: 45.8 us; the launch traced here: 45.4 us
  starting transfers between devices  31.8 us (69%)
  Pallas kernels  8.34 us (18%)
  blocking collectives  4.4 us (10%)
  waiting for transfers between devices  0.69 us (2%)
    ppermute x1, starting transfers between devices, shards(): first = lax.ppermute(row, 'zh', [(k, k ^ 1) for k in range(ZH)])  9.64 us
    all_to_all x1, starting transfers between devices, shards(): lax.all_to_all(col_sends, 'c', 0, 0, tiled=True, axis_index_groups=[C_ORD...  8.39 us
    ppermute x1, starting transfers between devices, crossed(): return lax.ppermute(array, ('zh', 'core'), swap)  7.52 us
    all_to_all x1, starting transfers between devices, shards(): lax.all_to_all(sends, 'y', 0, 0, tiled=True, axis_index_groups=[Y_ORDER])  6.3 us
    all_gather x1, blocking collectives, shards(): everything = lax.all_gather(over_y, 'core', axis=0, tiled=False)  4.4 us
    pallas_call x1, Pallas kernels, shards(): pl.pallas_call(left_kernel, in_specs=[vmem] * 3, out_specs=(vmem, vmem),...  2.31 us
    pallas_call x1, Pallas kernels, shards(): pl.pallas_call(schur_kernel, in_specs=[pl.BlockSpec(memory_space=pltpu.SM...  2.04 us
    pallas_call x1, Pallas kernels, shards(): pl.pallas_call(fetch_kernel, in_specs=[vmem, hbm], out_specs=(vmem,) * 4,...  1.57 us
  transfers between devices with their start and end apart: 4, of which 2 were waited for; matrix products, arithmetic and copies ran while one was open for 0% of the time, Pallas kernels for 12%

profile of v5, /device:TPU:1, one launch (start us, length us, event | category | flops | bytes accessed | tf_op | source)
XLA Modules:
  0.0 45.4 jit_solution(7726367580279973953)
XLA Ops:
  0.0 0.8 %pack.1 = (bf16[64,128]{1,0:T(8,128)(2,1)S(1)}, bf16[32,128]{1,0:T(8,128)(2,1)S(1)}) custom-call(bf16[4,16,64]{2,1,0:T(8,128)(2,1)} %ru_ref.1, bf16[4,16,64]{2,1,0:T(8,128)(2,1)} %rv_ref.1, bf16[1,32,64]{2,1,0:T(8,128)(2,1)} %cu_ref.1, bf16[1,32,64]{2,1,0:T(8,128)(2,1)} %cv_ref.1), custom_call_target="tpu_custom_call" | custom-call | tf_op jit(solution)/shard_map/pack/pallas_call | solution.py:135
  0.8 9.6 %collective-permute-start = (bf16[64,128]{1,0:T(8,128)(2,1)S(1)}, bf16[64,128]{1,0:T(8,128)(2,1)S(1)}, u32[]{:S(2)}, u32[]{:S(2)}) collective-permute-start(bf16[64,128]{1,0:T(8,128)(2,1)S(1)} %get-tuple-element.20.own_ref), channel_id=1, source_target_pairs={{0,32},{32,0},{64,96},{96,64},{1,33},{33,1},{65,97},{97,65},{2,34}... | collective-permute-start | bytes 49160 | tf_op jit(solution)/shard_map/ppermute | solution.py:153
  10.5 0.8 %spread.1 = bf16[16,32,128]{2,1,0:T(8,128)(2,1)} custom-call(bf16[32,128]{1,0:T(8,128)(2,1)S(1)} %get-tuple-element.26.col_ref), custom_call_target="tpu_custom_call" | custom-call | tf_op jit(solution)/shard_map/spread/pallas_call | solution.py:142
  11.3 8.4 %all-to-all-start = ((bf16[16,32,128]{2,1,0:T(8,128)(2,1)}), bf16[16,32,128]{2,1,0:T(8,128)(2,1)S(1)}, u32[]{:S(2)}, u32[]{:S(2)}) async-start(bf16[16,32,128]{2,1,0:T(8,128)(2,1)} %spread.1), calls=%async_computation | async-start | bytes 262144 | tf_op jit(solution)/shard_map/all_to_all | solution.py:150
  19.7 0.0 collective-permute-done.first_ref
  19.7 7.5 %collective-permute-start.1 = (bf16[2,64,128]{2,1,0:T(8,128)(2,1)S(1)}, bf16[2,64,128]{2,1,0:T(8,128)(2,1)S(1)}, u32[]{:S(2)}, u32[]{:S(2)}) collective-permute-start(bf16[2,64,128]{2,1,0:T(8,128)(2,1)S(1)} %pad_maximum_fusion.after_ref), channel_id=1, source_target_pairs={{0,112},{16,96},{32,80},{48,64},{64,48},{80,32},{96,16},{112,0},{1... | collective-permute-start | bytes 98312 | tf_op jit(solution)/shard_map/ppermute | solution.py:27
  27.2 1.6 %fetch.1 = (bf16[512,512]{1,0:T(8,128)(2,1)S(1)}, bf16[512,512]{1,0:T(8,128)(2,1)S(1)}, bf16[512,512]{1,0:T(8,128)(2,1)S(1)}, bf16[512,512]{1,0:T(8,128)(2,1)S(1)}) custom-call(bf16[2,64,128]{2,1,0:T(8,128)(2,1)S(1)} %pad_maximum_fusion.after_ref, bf16[512,2048]{1,0:T(8,128)(2,1)} %t_hbm.1), custom_call_target="tpu_custom_call" | custom-call | tf_op jit(solution)/shard_map/fetch/pallas_call | solution.py:156
  28.8 0.2 collective-permute-done.1.other_ref
  28.9 0.8 %fan.1 = bf16[4,4,64,128]{3,2,1,0:T(8,128)(2,1)} custom-call(bf16[64,128]{1,0:T(8,128)(2,1)S(1)} %get-tuple-element.20.own_ref, bf16[64,128]{1,0:T(8,128)(2,1)S(1)} %collective-permute-done.first_ref, bf16[2,64,128]{2,1,0:T(8,128)(2,1)S(1)} %collective-permute-done.1.other_ref), custom_call_target="tpu_custom_call" | custom-call | flops 4000000000 | bytes 262144 | tf_op jit(solution)/shard_map/fan/pallas_call | solution.py:166
  29.8 0.0 all-to-all-done.col_ref
  29.8 6.3 %all-to-all-start.1 = ((bf16[4,4,64,128]{3,2,1,0:T(8,128)(2,1)}), bf16[4,4,64,128]{3,2,1,0:T(8,128)(2,1)S(1)}, u32[]{:S(2)}, u32[]{:S(2)}) async-start(bf16[4,4,64,128]{3,2,1,0:T(8,128)(2,1)} %fan.1), calls=%async_computation.1 | async-start | bytes 524288 | tf_op jit(solution)/shard_map/all_to_all | solution.py:177
  36.1 2.3 %left.1 = (bf16[128,512]{1,0:T(8,128)(2,1)S(1)}, bf16[512,128]{1,0:T(8,128)(2,1)S(1)}) custom-call(bf16[16,32,128]{2,1,0:T(8,128)(2,1)S(1)} %all-to-all-done.col_ref, f32[512,512]{1,0:T(8,128)} %upper_ref.1, f32[512,512]{1,0:T(8,128)} %lower_ref.1), custom_call_target="tpu_custom_call" | custom-call | tf_op jit(solution)/shard_map/left/pallas_call | solution.py:179
  38.4 0.5 %all-to-all-done.1 = bf16[4,4,64,128]{3,2,1,0:T(8,128)(2,1)S(1)} async-done(((bf16[4,4,64,128]{3,2,1,0:T(8,128)(2,1)}), bf16[4,4,64,128]{3,2,1,0:T(8,128)(2,1)S(1)}, u32[]{:S(2)}, u32[]{:S(2)}) %all-to-all-start.1) | async-done | bytes 262176 | tf_op jit(solution)/shard_map/all_to_all | solution.py:177
  38.9 4.4 %all-gather = bf16[8,4,64,128]{3,2,1,0:T(8,128)(2,1)S(1)} all-gather(bf16[4,4,64,128]{3,2,1,0:T(8,128)(2,1)S(1)} %all-to-all-done.1), channel_id=2, replica_groups=mesh['y'=4,'zh'=4,'core'=2,'c'=16] {'core'}, dimensions={0}, use_global_device_ids=true | all-gather | bytes 786432 | tf_op jit(solution)/shard_map/all_gather | solution.py:178
  43.3 2.0 %schur.1 = bf16[512,2048]{1,0:T(8,128)(2,1)} custom-call(s32[1]{0:T(128)} %bitcast.me_ref, bf16[2,4,4,64,128]{4,3,2,1,0:T(8,128)(2,1)S(1)} %bitcast.4, bf16[128,512]{1,0:T(8,128)(2,1)S(1)} %get-tuple-element.29.q_ref, bf16[512,128]{1,0:T(8,128)(2,1)S(1)} %get-tuple-element.30.uu_ref, bf16[512,512]{1,0:T(8,128)(2,1)S(1)} %get-tuple-element.31.t0_ref, ...), custom_call_target="tpu_custom_call" | custom-call | tf_op jit(solution)/shard_map/schur/pallas_call | solution.py:187
  (1 shorter events, 0.0 us)
Async XLA Ops:
  0.8 18.9 %collective-permute-start = (bf16[64,128]{1,0:T(8,128)(2,1)S(1)}, bf16[64,128]{1,0:T(8,128)(2,1)S(1)}, u32[]{:S(2)}, u32[]{:S(2)}) collective-permute-start(bf16[64,128]{1,0:T(8,128)(2,1)S(1)} %get-tuple-element.20.own_ref), channel_id=1, source_target_pairs={{0,32},{32,0},{64,96},{96,64},{1,33},{33,1},{65,97},{97,65},{2,34}... | collective-permute-start | bytes 49160 | tf_op jit(solution)/shard_map/ppermute | solution.py:153
  11.3 18.5 %all-to-all-start = ((bf16[16,32,128]{2,1,0:T(8,128)(2,1)}), bf16[16,32,128]{2,1,0:T(8,128)(2,1)S(1)}, u32[]{:S(2)}, u32[]{:S(2)}) async-start(bf16[16,32,128]{2,1,0:T(8,128)(2,1)} %spread.1), calls=%async_computation | async-start | bytes 262144 | tf_op jit(solution)/shard_map/all_to_all | solution.py:150
  19.7 9.3 %collective-permute-start.1 = (bf16[2,64,128]{2,1,0:T(8,128)(2,1)S(1)}, bf16[2,64,128]{2,1,0:T(8,128)(2,1)S(1)}, u32[]{:S(2)}, u32[]{:S(2)}) collective-permute-start(bf16[2,64,128]{2,1,0:T(8,128)(2,1)S(1)} %pad_maximum_fusion.after_ref), channel_id=1, source_target_pairs={{0,112},{16,96},{32,80},{48,64},{64,48},{80,32},{96,16},{112,0},{1... | collective-permute-start | bytes 98312 | tf_op jit(solution)/shard_map/ppermute | solution.py:27
  29.8 9.1 %all-to-all-start.1 = ((bf16[4,4,64,128]{3,2,1,0:T(8,128)(2,1)}), bf16[4,4,64,128]{3,2,1,0:T(8,128)(2,1)S(1)}, u32[]{:S(2)}, u32[]{:S(2)}) async-start(bf16[4,4,64,128]{3,2,1,0:T(8,128)(2,1)} %fan.1), calls=%async_computation.1 | async-start | bytes 524288 | tf_op jit(solution)/shard_map/all_to_all | solution.py:177

commit v6 on v5

--- a/solution.py
+++ b/solution.py
@@ -7,7 +7,7 @@
 
 Y, ZH, CORE, C = 4, 4, 2, 16
 ROW, COL = ("y", "zh", "core"), ("c",)
-Y_ORDER = [2, 3, 0, 1]
+Y_ORDER = [2, 0, 3, 1]
 C_ORDER = [4, *[c for c in range(C) if c != 4]]
 B, R = 512, 64
 F32, BF16 = jnp.float32, jnp.bfloat16

time: 45.8 us -> 45.2 us (0.987)
  no operation moved by 1% of the time
where the time goes in v6:
time: 45.2 us; the launch traced here: 44.8 us
  starting transfers between devices  31.8 us (70%)
  Pallas kernels  8.34 us (18%)
  blocking collectives  4.12 us (9%)
    ppermute x1, starting transfers between devices, shards(): first = lax.ppermute(row, 'zh', [(k, k ^ 1) for k in range(ZH)])  9.64 us
    all_to_all x1, starting transfers between devices, shards(): lax.all_to_all(col_sends, 'c', 0, 0, tiled=True, axis_index_groups=[C_ORD...  8.39 us
    ppermute x1, starting transfers between devices, crossed(): return lax.ppermute(array, ('zh', 'core'), swap)  7.52 us
    all_to_all x1, starting transfers between devices, shards(): lax.all_to_all(sends, 'y', 0, 0, tiled=True, axis_index_groups=[Y_ORDER])  6.3 us
    all_gather x1, blocking collectives, shards(): everything = lax.all_gather(over_y, 'core', axis=0, tiled=False)  4.12 us
    pallas_call x1, Pallas kernels, shards(): pl.pallas_call(left_kernel, in_specs=[vmem] * 3, out_specs=(vmem, vmem),...  2.31 us
    pallas_call x1, Pallas kernels, shards(): pl.pallas_call(schur_kernel, in_specs=[pl.BlockSpec(memory_space=pltpu.SM...  2.04 us
    pallas_call x1, Pallas kernels, shards(): pl.pallas_call(fetch_kernel, in_specs=[vmem, hbm], out_specs=(vmem,) * 4,...  1.57 us
  transfers between devices with their start and end apart: 4, of which 2 were waited for; matrix products, arithmetic and copies ran while one was open for 0% of the time, Pallas kernels for 12%

profile of v6, /device:TPU:1, one launch (start us, length us, event | category | flops | bytes accessed | tf_op | source)
XLA Modules:
  0.0 44.8 jit_solution(10492707347222422228)
XLA Ops:
  0.0 0.8 %pack.1 = (bf16[64,128]{1,0:T(8,128)(2,1)S(1)}, bf16[32,128]{1,0:T(8,128)(2,1)S(1)}) custom-call(bf16[4,16,64]{2,1,0:T(8,128)(2,1)} %ru_ref.1, bf16[4,16,64]{2,1,0:T(8,128)(2,1)} %rv_ref.1, bf16[1,32,64]{2,1,0:T(8,128)(2,1)} %cu_ref.1, bf16[1,32,64]{2,1,0:T(8,128)(2,1)} %cv_ref.1), custom_call_target="tpu_custom_call" | custom-call | tf_op jit(solution)/shard_map/pack/pallas_call | solution.py:135
  0.8 9.6 %collective-permute-start = (bf16[64,128]{1,0:T(8,128)(2,1)S(1)}, bf16[64,128]{1,0:T(8,128)(2,1)S(1)}, u32[]{:S(2)}, u32[]{:S(2)}) collective-permute-start(bf16[64,128]{1,0:T(8,128)(2,1)S(1)} %get-tuple-element.20.own_ref), channel_id=1, source_target_pairs={{0,32},{32,0},{64,96},{96,64},{1,33},{33,1},{65,97},{97,65},{2,34}... | collective-permute-start | bytes 49160 | tf_op jit(solution)/shard_map/ppermute | solution.py:153
  10.5 0.8 %spread.1 = bf16[16,32,128]{2,1,0:T(8,128)(2,1)} custom-call(bf16[32,128]{1,0:T(8,128)(2,1)S(1)} %get-tuple-element.26.col_ref), custom_call_target="tpu_custom_call" | custom-call | tf_op jit(solution)/shard_map/spread/pallas_call | solution.py:142
  11.3 8.4 %all-to-all-start = ((bf16[16,32,128]{2,1,0:T(8,128)(2,1)}), bf16[16,32,128]{2,1,0:T(8,128)(2,1)S(1)}, u32[]{:S(2)}, u32[]{:S(2)}) async-start(bf16[16,32,128]{2,1,0:T(8,128)(2,1)} %spread.1), calls=%async_computation | async-start | bytes 262144 | tf_op jit(solution)/shard_map/all_to_all | solution.py:150
  19.7 0.0 collective-permute-done.first_ref
  19.7 7.5 %collective-permute-start.1 = (bf16[2,64,128]{2,1,0:T(8,128)(2,1)S(1)}, bf16[2,64,128]{2,1,0:T(8,128)(2,1)S(1)}, u32[]{:S(2)}, u32[]{:S(2)}) collective-permute-start(bf16[2,64,128]{2,1,0:T(8,128)(2,1)S(1)} %pad_maximum_fusion.after_ref), channel_id=1, source_target_pairs={{0,112},{16,96},{32,80},{48,64},{64,48},{80,32},{96,16},{112,0},{1... | collective-permute-start | bytes 98312 | tf_op jit(solution)/shard_map/ppermute | solution.py:27
  27.2 1.6 %fetch.1 = (bf16[512,512]{1,0:T(8,128)(2,1)S(1)}, bf16[512,512]{1,0:T(8,128)(2,1)S(1)}, bf16[512,512]{1,0:T(8,128)(2,1)S(1)}, bf16[512,512]{1,0:T(8,128)(2,1)S(1)}) custom-call(bf16[2,64,128]{2,1,0:T(8,128)(2,1)S(1)} %pad_maximum_fusion.after_ref, bf16[512,2048]{1,0:T(8,128)(2,1)} %t_hbm.1), custom_call_target="tpu_custom_call" | custom-call | tf_op jit(solution)/shard_map/fetch/pallas_call | solution.py:156
  28.8 0.2 collective-permute-done.1.other_ref
  28.9 0.8 %fan.1 = bf16[4,4,64,128]{3,2,1,0:T(8,128)(2,1)} custom-call(bf16[64,128]{1,0:T(8,128)(2,1)S(1)} %get-tuple-element.20.own_ref, bf16[64,128]{1,0:T(8,128)(2,1)S(1)} %collective-permute-done.first_ref, bf16[2,64,128]{2,1,0:T(8,128)(2,1)S(1)} %collective-permute-done.1.other_ref), custom_call_target="tpu_custom_call" | custom-call | flops 4000000000 | bytes 262144 | tf_op jit(solution)/shard_map/fan/pallas_call | solution.py:166
  29.8 0.0 all-to-all-done.col_ref
  29.8 6.3 %all-to-all-start.1 = ((bf16[4,4,64,128]{3,2,1,0:T(8,128)(2,1)}), bf16[4,4,64,128]{3,2,1,0:T(8,128)(2,1)S(1)}, u32[]{:S(2)}, u32[]{:S(2)}) async-start(bf16[4,4,64,128]{3,2,1,0:T(8,128)(2,1)} %fan.1), calls=%async_computation.1 | async-start | bytes 524288 | tf_op jit(solution)/shard_map/all_to_all | solution.py:177
  36.1 2.3 %left.1 = (bf16[128,512]{1,0:T(8,128)(2,1)S(1)}, bf16[512,128]{1,0:T(8,128)(2,1)S(1)}) custom-call(bf16[16,32,128]{2,1,0:T(8,128)(2,1)S(1)} %all-to-all-done.col_ref, f32[512,512]{1,0:T(8,128)} %upper_ref.1, f32[512,512]{1,0:T(8,128)} %lower_ref.1), custom_call_target="tpu_custom_call" | custom-call | tf_op jit(solution)/shard_map/left/pallas_call | solution.py:179
  38.4 0.3 all-to-all-done.1
  38.6 4.1 %all-gather = bf16[8,4,64,128]{3,2,1,0:T(8,128)(2,1)S(1)} all-gather(bf16[4,4,64,128]{3,2,1,0:T(8,128)(2,1)S(1)} %all-to-all-done.1), channel_id=2, replica_groups=mesh['y'=4,'zh'=4,'core'=2,'c'=16] {'core'}, dimensions={0}, use_global_device_ids=true | all-gather | bytes 786432 | tf_op jit(solution)/shard_map/all_gather | solution.py:178
  42.8 2.0 %schur.1 = bf16[512,2048]{1,0:T(8,128)(2,1)} custom-call(s32[1]{0:T(128)} %bitcast.me_ref, bf16[2,4,4,64,128]{4,3,2,1,0:T(8,128)(2,1)S(1)} %bitcast.4, bf16[128,512]{1,0:T(8,128)(2,1)S(1)} %get-tuple-element.29.q_ref, bf16[512,128]{1,0:T(8,128)(2,1)S(1)} %get-tuple-element.30.uu_ref, bf16[512,512]{1,0:T(8,128)(2,1)S(1)} %get-tuple-element.31.t0_ref, ...), custom_call_target="tpu_custom_call" | custom-call | tf_op jit(solution)/shard_map/schur/pallas_call | solution.py:187
  (1 shorter events, 0.0 us)
Async XLA Ops:
  0.8 18.9 %collective-permute-start = (bf16[64,128]{1,0:T(8,128)(2,1)S(1)}, bf16[64,128]{1,0:T(8,128)(2,1)S(1)}, u32[]{:S(2)}, u32[]{:S(2)}) collective-permute-start(bf16[64,128]{1,0:T(8,128)(2,1)S(1)} %get-tuple-element.20.own_ref), channel_id=1, source_target_pairs={{0,32},{32,0},{64,96},{96,64},{1,33},{33,1},{65,97},{97,65},{2,34}... | collective-permute-start | bytes 49160 | tf_op jit(solution)/shard_map/ppermute | solution.py:153
  11.3 18.5 %all-to-all-start = ((bf16[16,32,128]{2,1,0:T(8,128)(2,1)}), bf16[16,32,128]{2,1,0:T(8,128)(2,1)S(1)}, u32[]{:S(2)}, u32[]{:S(2)}) async-start(bf16[16,32,128]{2,1,0:T(8,128)(2,1)} %spread.1), calls=%async_computation | async-start | bytes 262144 | tf_op jit(solution)/shard_map/all_to_all | solution.py:150
  19.7 9.3 %collective-permute-start.1 = (bf16[2,64,128]{2,1,0:T(8,128)(2,1)S(1)}, bf16[2,64,128]{2,1,0:T(8,128)(2,1)S(1)}, u32[]{:S(2)}, u32[]{:S(2)}) collective-permute-start(bf16[2,64,128]{2,1,0:T(8,128)(2,1)S(1)} %pad_maximum_fusion.after_ref), channel_id=1, source_target_pairs={{0,112},{16,96},{32,80},{48,64},{64,48},{80,32},{96,16},{112,0},{1... | collective-permute-start | bytes 98312 | tf_op jit(solution)/shard_map/ppermute | solution.py:27
  29.8 8.9 %all-to-all-start.1 = ((bf16[4,4,64,128]{3,2,1,0:T(8,128)(2,1)}), bf16[4,4,64,128]{3,2,1,0:T(8,128)(2,1)S(1)}, u32[]{:S(2)}, u32[]{:S(2)}) async-start(bf16[4,4,64,128]{3,2,1,0:T(8,128)(2,1)} %fan.1), calls=%async_computation.1 | async-start | bytes 524288 | tf_op jit(solution)/shard_map/all_to_all | solution.py:177

commit v7 on v6

--- a/solution.py
+++ b/solution.py
@@ -108,12 +108,17 @@
         ws.append(jnp.concatenate(split(w[:R] + w[R:]), axis=0))
     uu = uu_ref[...]
     stores = []
+    rows = B // 4
     for j in range(tiles):
-        p = dot(uu, ws[j])
-        obuf[j] = (held[j][...].astype(F32) - p).astype(BF16)
-        s = pltpu.make_async_copy(obuf.at[j], o_hbm.at[:, pl.ds(j * B, B)], osem.at[j])
-        s.start()
-        stores.append(s)
+        for i in range(4):
+            part = pl.ds(i * rows, rows)
+            p = dot(uu[i * rows : (i + 1) * rows], ws[j])
+            obuf[j, part] = (held[j][part, :].astype(F32) - p).astype(BF16)
+            s = pltpu.make_async_copy(
+                obuf.at[j, part], o_hbm.at[part, pl.ds(j * B, B)], osem.at[j, i]
+            )
+            s.start()
+            stores.append(s)
     for s in stores:
         s.wait()
 
@@ -191,7 +196,7 @@
         out_shape=jax.ShapeDtypeStruct((B, 4 * B), BF16),
         scratch_shapes=[
             pltpu.VMEM((4, B, B), BF16),
-            pltpu.SemaphoreType.DMA((4,)),
+            pltpu.SemaphoreType.DMA((4, 4)),
         ],
         name="schur",
     )(lax.axis_index("zh")[None], *on_chip(everything.reshape(CORE, Y, ZH, 64, 128), q, uu, *held))

time: 45.2 us -> 45.2 us (level)
  no operation moved by 1% of the time
where the time goes in v7:
time: 45.2 us; the launch traced here: 44.8 us
  starting transfers between devices  31.8 us (70%)
  Pallas kernels  8.34 us (18%)
  blocking collectives  4.12 us (9%)
    ppermute x1, starting transfers between devices, shards(): first = lax.ppermute(row, 'zh', [(k, k ^ 1) for k in range(ZH)])  9.64 us
    all_to_all x1, starting transfers between devices, shards(): lax.all_to_all(col_sends, 'c', 0, 0, tiled=True, axis_index_groups=[C_ORD...  8.39 us
    ppermute x1, starting transfers between devices, crossed(): return lax.ppermute(array, ('zh', 'core'), swap)  7.52 us
    all_to_all x1, starting transfers between devices, shards(): lax.all_to_all(sends, 'y', 0, 0, tiled=True, axis_index_groups=[Y_ORDER])  6.3 us
    all_gather x1, blocking collectives, shards(): everything = lax.all_gather(over_y, 'core', axis=0, tiled=False)  4.12 us
    pallas_call x1, Pallas kernels, shards(): pl.pallas_call(left_kernel, in_specs=[vmem] * 3, out_specs=(vmem, vmem),...  2.31 us
    pallas_call x1, Pallas kernels, shards(): pl.pallas_call(schur_kernel, in_specs=[pl.BlockSpec(memory_space=pltpu.SM...  2.04 us
    pallas_call x1, Pallas kernels, shards(): pl.pallas_call(fetch_kernel, in_specs=[vmem, hbm], out_specs=(vmem,) * 4,...  1.57 us
  transfers between devices with their start and end apart: 4, of which 2 were waited for; matrix products, arithmetic and copies ran while one was open for 0% of the time, Pallas kernels for 12%

profile of v7, /device:TPU:1, one launch (start us, length us, event | category | flops | bytes accessed | tf_op | source)
XLA Modules:
  0.0 44.8 jit_solution(10746768122518934232)
XLA Ops:
  0.0 0.8 %pack.1 = (bf16[64,128]{1,0:T(8,128)(2,1)S(1)}, bf16[32,128]{1,0:T(8,128)(2,1)S(1)}) custom-call(bf16[4,16,64]{2,1,0:T(8,128)(2,1)} %ru_ref.1, bf16[4,16,64]{2,1,0:T(8,128)(2,1)} %rv_ref.1, bf16[1,32,64]{2,1,0:T(8,128)(2,1)} %cu_ref.1, bf16[1,32,64]{2,1,0:T(8,128)(2,1)} %cv_ref.1), custom_call_target="tpu_custom_call" | custom-call | tf_op jit(solution)/shard_map/pack/pallas_call | solution.py:140
  0.8 9.6 %collective-permute-start = (bf16[64,128]{1,0:T(8,128)(2,1)S(1)}, bf16[64,128]{1,0:T(8,128)(2,1)S(1)}, u32[]{:S(2)}, u32[]{:S(2)}) collective-permute-start(bf16[64,128]{1,0:T(8,128)(2,1)S(1)} %get-tuple-element.20.own_ref), channel_id=1, source_target_pairs={{0,32},{32,0},{64,96},{96,64},{1,33},{33,1},{65,97},{97,65},{2,34}... | collective-permute-start | bytes 49160 | tf_op jit(solution)/shard_map/ppermute | solution.py:158
  10.5 0.8 %spread.1 = bf16[16,32,128]{2,1,0:T(8,128)(2,1)} custom-call(bf16[32,128]{1,0:T(8,128)(2,1)S(1)} %get-tuple-element.26.col_ref), custom_call_target="tpu_custom_call" | custom-call | tf_op jit(solution)/shard_map/spread/pallas_call | solution.py:147
  11.3 8.4 %all-to-all-start = ((bf16[16,32,128]{2,1,0:T(8,128)(2,1)}), bf16[16,32,128]{2,1,0:T(8,128)(2,1)S(1)}, u32[]{:S(2)}, u32[]{:S(2)}) async-start(bf16[16,32,128]{2,1,0:T(8,128)(2,1)} %spread.1), calls=%async_computation | async-start | bytes 262144 | tf_op jit(solution)/shard_map/all_to_all | solution.py:155
  19.7 0.0 collective-permute-done.first_ref
  19.7 7.5 %collective-permute-start.1 = (bf16[2,64,128]{2,1,0:T(8,128)(2,1)S(1)}, bf16[2,64,128]{2,1,0:T(8,128)(2,1)S(1)}, u32[]{:S(2)}, u32[]{:S(2)}) collective-permute-start(bf16[2,64,128]{2,1,0:T(8,128)(2,1)S(1)} %pad_maximum_fusion.after_ref), channel_id=1, source_target_pairs={{0,112},{16,96},{32,80},{48,64},{64,48},{80,32},{96,16},{112,0},{1... | collective-permute-start | bytes 98312 | tf_op jit(solution)/shard_map/ppermute | solution.py:27
  27.2 1.6 %fetch.1 = (bf16[512,512]{1,0:T(8,128)(2,1)S(1)}, bf16[512,512]{1,0:T(8,128)(2,1)S(1)}, bf16[512,512]{1,0:T(8,128)(2,1)S(1)}, bf16[512,512]{1,0:T(8,128)(2,1)S(1)}) custom-call(bf16[2,64,128]{2,1,0:T(8,128)(2,1)S(1)} %pad_maximum_fusion.after_ref, bf16[512,2048]{1,0:T(8,128)(2,1)} %t_hbm.1), custom_call_target="tpu_custom_call" | custom-call | tf_op jit(solution)/shard_map/fetch/pallas_call | solution.py:161
  28.8 0.2 collective-permute-done.1.other_ref
  28.9 0.8 %fan.1 = bf16[4,4,64,128]{3,2,1,0:T(8,128)(2,1)} custom-call(bf16[64,128]{1,0:T(8,128)(2,1)S(1)} %get-tuple-element.20.own_ref, bf16[64,128]{1,0:T(8,128)(2,1)S(1)} %collective-permute-done.first_ref, bf16[2,64,128]{2,1,0:T(8,128)(2,1)S(1)} %collective-permute-done.1.other_ref), custom_call_target="tpu_custom_call" | custom-call | flops 4000000000 | bytes 262144 | tf_op jit(solution)/shard_map/fan/pallas_call | solution.py:171
  29.8 0.0 all-to-all-done.col_ref
  29.8 6.3 %all-to-all-start.1 = ((bf16[4,4,64,128]{3,2,1,0:T(8,128)(2,1)}), bf16[4,4,64,128]{3,2,1,0:T(8,128)(2,1)S(1)}, u32[]{:S(2)}, u32[]{:S(2)}) async-start(bf16[4,4,64,128]{3,2,1,0:T(8,128)(2,1)} %fan.1), calls=%async_computation.1 | async-start | bytes 524288 | tf_op jit(solution)/shard_map/all_to_all | solution.py:182
  36.1 2.3 %left.1 = (bf16[128,512]{1,0:T(8,128)(2,1)S(1)}, bf16[512,128]{1,0:T(8,128)(2,1)S(1)}) custom-call(bf16[16,32,128]{2,1,0:T(8,128)(2,1)S(1)} %all-to-all-done.col_ref, f32[512,512]{1,0:T(8,128)} %upper_ref.1, f32[512,512]{1,0:T(8,128)} %lower_ref.1), custom_call_target="tpu_custom_call" | custom-call | tf_op jit(solution)/shard_map/left/pallas_call | solution.py:184
  38.4 0.3 all-to-all-done.1
  38.6 4.1 %all-gather = bf16[8,4,64,128]{3,2,1,0:T(8,128)(2,1)S(1)} all-gather(bf16[4,4,64,128]{3,2,1,0:T(8,128)(2,1)S(1)} %all-to-all-done.1), channel_id=2, replica_groups=mesh['y'=4,'zh'=4,'core'=2,'c'=16] {'core'}, dimensions={0}, use_global_device_ids=true | all-gather | bytes 786432 | tf_op jit(solution)/shard_map/all_gather | solution.py:183
  42.8 2.0 %schur.1 = bf16[512,2048]{1,0:T(8,128)(2,1)} custom-call(s32[1]{0:T(128)} %bitcast.me_ref, bf16[2,4,4,64,128]{4,3,2,1,0:T(8,128)(2,1)S(1)} %bitcast.4, bf16[128,512]{1,0:T(8,128)(2,1)S(1)} %get-tuple-element.29.q_ref, bf16[512,128]{1,0:T(8,128)(2,1)S(1)} %get-tuple-element.30.uu_ref, bf16[512,512]{1,0:T(8,128)(2,1)S(1)} %get-tuple-element.31.t0_ref, ...), custom_call_target="tpu_custom_call" | custom-call | tf_op jit(solution)/shard_map/schur/pallas_call | solution.py:192
  (1 shorter events, 0.0 us)
Async XLA Ops:
  0.8 18.9 %collective-permute-start = (bf16[64,128]{1,0:T(8,128)(2,1)S(1)}, bf16[64,128]{1,0:T(8,128)(2,1)S(1)}, u32[]{:S(2)}, u32[]{:S(2)}) collective-permute-start(bf16[64,128]{1,0:T(8,128)(2,1)S(1)} %get-tuple-element.20.own_ref), channel_id=1, source_target_pairs={{0,32},{32,0},{64,96},{96,64},{1,33},{33,1},{65,97},{97,65},{2,34}... | collective-permute-start | bytes 49160 | tf_op jit(solution)/shard_map/ppermute | solution.py:158
  11.3 18.5 %all-to-all-start = ((bf16[16,32,128]{2,1,0:T(8,128)(2,1)}), bf16[16,32,128]{2,1,0:T(8,128)(2,1)S(1)}, u32[]{:S(2)}, u32[]{:S(2)}) async-start(bf16[16,32,128]{2,1,0:T(8,128)(2,1)} %spread.1), calls=%async_computation | async-start | bytes 262144 | tf_op jit(solution)/shard_map/all_to_all | solution.py:155
  19.7 9.3 %collective-permute-start.1 = (bf16[2,64,128]{2,1,0:T(8,128)(2,1)S(1)}, bf16[2,64,128]{2,1,0:T(8,128)(2,1)S(1)}, u32[]{:S(2)}, u32[]{:S(2)}) collective-permute-start(bf16[2,64,128]{2,1,0:T(8,128)(2,1)S(1)} %pad_maximum_fusion.after_ref), channel_id=1, source_target_pairs={{0,112},{16,96},{32,80},{48,64},{64,48},{80,32},{96,16},{112,0},{1... | collective-permute-start | bytes 98312 | tf_op jit(solution)/shard_map/ppermute | solution.py:27
  29.8 8.9 %all-to-all-start.1 = ((bf16[4,4,64,128]{3,2,1,0:T(8,128)(2,1)}), bf16[4,4,64,128]{3,2,1,0:T(8,128)(2,1)S(1)}, u32[]{:S(2)}, u32[]{:S(2)}) async-start(bf16[4,4,64,128]{3,2,1,0:T(8,128)(2,1)} %fan.1), calls=%async_computation.1 | async-start | bytes 524288 | tf_op jit(solution)/shard_map/all_to_all | solution.py:182

commit v8 on v7

--- a/solution.py
+++ b/solution.py
@@ -7,7 +7,7 @@
 
 Y, ZH, CORE, C = 4, 4, 2, 16
 ROW, COL = ("y", "zh", "core"), ("c",)
-Y_ORDER = [2, 0, 3, 1]
+Y_ORDER = [2, 0, 1, 3]
 C_ORDER = [4, *[c for c in range(C) if c != 4]]
 B, R = 512, 64
 F32, BF16 = jnp.float32, jnp.bfloat16

time: 45.2 us -> 45.2 us (level)
  no operation moved by 1% of the time
where the time goes in v8:
time: 45.2 us; the launch traced here: 44.8 us
  starting transfers between devices  31.8 us (70%)
  Pallas kernels  8.34 us (18%)
  blocking collectives  4.12 us (9%)
    ppermute x1, starting transfers between devices, shards(): first = lax.ppermute(row, 'zh', [(k, k ^ 1) for k in range(ZH)])  9.64 us
    all_to_all x1, starting transfers between devices, shards(): lax.all_to_all(col_sends, 'c', 0, 0, tiled=True, axis_index_groups=[C_ORD...  8.39 us
    ppermute x1, starting transfers between devices, crossed(): return lax.ppermute(array, ('zh', 'core'), swap)  7.52 us
    all_to_all x1, starting transfers between devices, shards(): lax.all_to_all(sends, 'y', 0, 0, tiled=True, axis_index_groups=[Y_ORDER])  6.3 us
    all_gather x1, blocking collectives, shards(): everything = lax.all_gather(over_y, 'core', axis=0, tiled=False)  4.12 us
    pallas_call x1, Pallas kernels, shards(): pl.pallas_call(left_kernel, in_specs=[vmem] * 3, out_specs=(vmem, vmem),...  2.31 us
    pallas_call x1, Pallas kernels, shards(): pl.pallas_call(schur_kernel, in_specs=[pl.BlockSpec(memory_space=pltpu.SM...  2.04 us
    pallas_call x1, Pallas kernels, shards(): pl.pallas_call(fetch_kernel, in_specs=[vmem, hbm], out_specs=(vmem,) * 4,...  1.57 us
  transfers between devices with their start and end apart: 4, of which 2 were waited for; matrix products, arithmetic and copies ran while one was open for 0% of the time, Pallas kernels for 12%

profile of v8, /device:TPU:1, one launch (start us, length us, event | category | flops | bytes accessed | tf_op | source)
XLA Modules:
  0.0 44.8 jit_solution(1901060759668055366)
XLA Ops:
  0.0 0.8 %pack.1 = (bf16[64,128]{1,0:T(8,128)(2,1)S(1)}, bf16[32,128]{1,0:T(8,128)(2,1)S(1)}) custom-call(bf16[4,16,64]{2,1,0:T(8,128)(2,1)} %ru_ref.1, bf16[4,16,64]{2,1,0:T(8,128)(2,1)} %rv_ref.1, bf16[1,32,64]{2,1,0:T(8,128)(2,1)} %cu_ref.1, bf16[1,32,64]{2,1,0:T(8,128)(2,1)} %cv_ref.1), custom_call_target="tpu_custom_call" | custom-call | tf_op jit(solution)/shard_map/pack/pallas_call | solution.py:140
  0.8 9.6 %collective-permute-start = (bf16[64,128]{1,0:T(8,128)(2,1)S(1)}, bf16[64,128]{1,0:T(8,128)(2,1)S(1)}, u32[]{:S(2)}, u32[]{:S(2)}) collective-permute-start(bf16[64,128]{1,0:T(8,128)(2,1)S(1)} %get-tuple-element.20.own_ref), channel_id=1, source_target_pairs={{0,32},{32,0},{64,96},{96,64},{1,33},{33,1},{65,97},{97,65},{2,34}... | collective-permute-start | bytes 49160 | tf_op jit(solution)/shard_map/ppermute | solution.py:158
  10.5 0.8 %spread.1 = bf16[16,32,128]{2,1,0:T(8,128)(2,1)} custom-call(bf16[32,128]{1,0:T(8,128)(2,1)S(1)} %get-tuple-element.26.col_ref), custom_call_target="tpu_custom_call" | custom-call | tf_op jit(solution)/shard_map/spread/pallas_call | solution.py:147
  11.3 8.4 %all-to-all-start = ((bf16[16,32,128]{2,1,0:T(8,128)(2,1)}), bf16[16,32,128]{2,1,0:T(8,128)(2,1)S(1)}, u32[]{:S(2)}, u32[]{:S(2)}) async-start(bf16[16,32,128]{2,1,0:T(8,128)(2,1)} %spread.1), calls=%async_computation | async-start | bytes 262144 | tf_op jit(solution)/shard_map/all_to_all | solution.py:155
  19.7 0.0 collective-permute-done.first_ref
  19.7 7.5 %collective-permute-start.1 = (bf16[2,64,128]{2,1,0:T(8,128)(2,1)S(1)}, bf16[2,64,128]{2,1,0:T(8,128)(2,1)S(1)}, u32[]{:S(2)}, u32[]{:S(2)}) collective-permute-start(bf16[2,64,128]{2,1,0:T(8,128)(2,1)S(1)} %pad_maximum_fusion.after_ref), channel_id=1, source_target_pairs={{0,112},{16,96},{32,80},{48,64},{64,48},{80,32},{96,16},{112,0},{1... | collective-permute-start | bytes 98312 | tf_op jit(solution)/shard_map/ppermute | solution.py:27
  27.2 1.6 %fetch.1 = (bf16[512,512]{1,0:T(8,128)(2,1)S(1)}, bf16[512,512]{1,0:T(8,128)(2,1)S(1)}, bf16[512,512]{1,0:T(8,128)(2,1)S(1)}, bf16[512,512]{1,0:T(8,128)(2,1)S(1)}) custom-call(bf16[2,64,128]{2,1,0:T(8,128)(2,1)S(1)} %pad_maximum_fusion.after_ref, bf16[512,2048]{1,0:T(8,128)(2,1)} %t_hbm.1), custom_call_target="tpu_custom_call" | custom-call | tf_op jit(solution)/shard_map/fetch/pallas_call | solution.py:161
  28.8 0.2 collective-permute-done.1.other_ref
  28.9 0.8 %fan.1 = bf16[4,4,64,128]{3,2,1,0:T(8,128)(2,1)} custom-call(bf16[64,128]{1,0:T(8,128)(2,1)S(1)} %get-tuple-element.20.own_ref, bf16[64,128]{1,0:T(8,128)(2,1)S(1)} %collective-permute-done.first_ref, bf16[2,64,128]{2,1,0:T(8,128)(2,1)S(1)} %collective-permute-done.1.other_ref), custom_call_target="tpu_custom_call" | custom-call | flops 4000000000 | bytes 262144 | tf_op jit(solution)/shard_map/fan/pallas_call | solution.py:171
  29.8 0.0 all-to-all-done.col_ref
  29.8 6.3 %all-to-all-start.1 = ((bf16[4,4,64,128]{3,2,1,0:T(8,128)(2,1)}), bf16[4,4,64,128]{3,2,1,0:T(8,128)(2,1)S(1)}, u32[]{:S(2)}, u32[]{:S(2)}) async-start(bf16[4,4,64,128]{3,2,1,0:T(8,128)(2,1)} %fan.1), calls=%async_computation.1 | async-start | bytes 524288 | tf_op jit(solution)/shard_map/all_to_all | solution.py:182
  36.1 2.3 %left.1 = (bf16[128,512]{1,0:T(8,128)(2,1)S(1)}, bf16[512,128]{1,0:T(8,128)(2,1)S(1)}) custom-call(bf16[16,32,128]{2,1,0:T(8,128)(2,1)S(1)} %all-to-all-done.col_ref, f32[512,512]{1,0:T(8,128)} %upper_ref.1, f32[512,512]{1,0:T(8,128)} %lower_ref.1), custom_call_target="tpu_custom_call" | custom-call | tf_op jit(solution)/shard_map/left/pallas_call | solution.py:184
  38.4 0.3 all-to-all-done.1
  38.6 4.1 %all-gather = bf16[8,4,64,128]{3,2,1,0:T(8,128)(2,1)S(1)} all-gather(bf16[4,4,64,128]{3,2,1,0:T(8,128)(2,1)S(1)} %all-to-all-done.1), channel_id=2, replica_groups=mesh['y'=4,'zh'=4,'core'=2,'c'=16] {'core'}, dimensions={0}, use_global_device_ids=true | all-gather | bytes 786432 | tf_op jit(solution)/shard_map/all_gather | solution.py:183
  42.8 2.0 %schur.1 = bf16[512,2048]{1,0:T(8,128)(2,1)} custom-call(s32[1]{0:T(128)} %bitcast.me_ref, bf16[2,4,4,64,128]{4,3,2,1,0:T(8,128)(2,1)S(1)} %bitcast.4, bf16[128,512]{1,0:T(8,128)(2,1)S(1)} %get-tuple-element.29.q_ref, bf16[512,128]{1,0:T(8,128)(2,1)S(1)} %get-tuple-element.30.uu_ref, bf16[512,512]{1,0:T(8,128)(2,1)S(1)} %get-tuple-element.31.t0_ref, ...), custom_call_target="tpu_custom_call" | custom-call | tf_op jit(solution)/shard_map/schur/pallas_call | solution.py:192
  (1 shorter events, 0.0 us)
Async XLA Ops:
  0.8 18.9 %collective-permute-start = (bf16[64,128]{1,0:T(8,128)(2,1)S(1)}, bf16[64,128]{1,0:T(8,128)(2,1)S(1)}, u32[]{:S(2)}, u32[]{:S(2)}) collective-permute-start(bf16[64,128]{1,0:T(8,128)(2,1)S(1)} %get-tuple-element.20.own_ref), channel_id=1, source_target_pairs={{0,32},{32,0},{64,96},{96,64},{1,33},{33,1},{65,97},{97,65},{2,34}... | collective-permute-start | bytes 49160 | tf_op jit(solution)/shard_map/ppermute | solution.py:158
  11.3 18.5 %all-to-all-start = ((bf16[16,32,128]{2,1,0:T(8,128)(2,1)}), bf16[16,32,128]{2,1,0:T(8,128)(2,1)S(1)}, u32[]{:S(2)}, u32[]{:S(2)}) async-start(bf16[16,32,128]{2,1,0:T(8,128)(2,1)} %spread.1), calls=%async_computation | async-start | bytes 262144 | tf_op jit(solution)/shard_map/all_to_all | solution.py:155
  19.7 9.3 %collective-permute-start.1 = (bf16[2,64,128]{2,1,0:T(8,128)(2,1)S(1)}, bf16[2,64,128]{2,1,0:T(8,128)(2,1)S(1)}, u32[]{:S(2)}, u32[]{:S(2)}) collective-permute-start(bf16[2,64,128]{2,1,0:T(8,128)(2,1)S(1)} %pad_maximum_fusion.after_ref), channel_id=1, source_target_pairs={{0,112},{16,96},{32,80},{48,64},{64,48},{80,32},{96,16},{112,0},{1... | collective-permute-start | bytes 98312 | tf_op jit(solution)/shard_map/ppermute | solution.py:27
  29.8 8.9 %all-to-all-start.1 = ((bf16[4,4,64,128]{3,2,1,0:T(8,128)(2,1)}), bf16[4,4,64,128]{3,2,1,0:T(8,128)(2,1)S(1)}, u32[]{:S(2)}, u32[]{:S(2)}) async-start(bf16[4,4,64,128]{3,2,1,0:T(8,128)(2,1)} %fan.1), calls=%async_computation.1 | async-start | bytes 524288 | tf_op jit(solution)/shard_map/all_to_all | solution.py:182
